TPU v7x, 256 devices: a whole 4x4x8 slice. The times are simulated.
256 devices in a mesh: pp: 2 (over x_hi), dp: 8 (over y, core), cp: 16 (over z, x_lo).
Axes of the slice: x: 4 (x_hi: 2, x_lo: 2; x = x_hi * 2 + x_lo), y: 4, z: 8, core: 2. Of those that a mesh axis runs over, the one named last changes fastest.
Arguments:
- tokens: bfloat16 [2, 2048, 3584], P('pp', 'cp'), may hold values from -6 to 6
- out_grad: bfloat16 [2, 2048, 3584], P('pp', 'cp'), may hold values from -6 to 6
- probs: bfloat16 [2, 2048, 8], P('pp', 'cp'), may hold values from 0.019897461 to 0.29882812
- expert_ids: int32 [2, 2048, 8], P('pp', 'cp'), may hold values from 0 to 15, all different within a row; in each aligned block of 128 rows (0 to 127, 128 to 255, ..., all dimensions but the last counted through in order) at most 80 rows name the same one
- w_gate: bfloat16 [2, 16, 1280, 3584], P('pp', 'cp', 'dp'), may hold values from -0.09375 to 0.09375
- w_up: bfloat16 [2, 16, 1280, 3584], P('pp', 'cp', 'dp'), may hold values from -0.09375 to 0.09375
- w_down: bfloat16 [2, 16, 1280, 3584], P('pp', 'cp', 'dp'), may hold values from -0.15625 to 0.15625
Outputs:
- passed_grad: bfloat16 [2, 2048, 3584], P('pp', 'cp', 'dp')
- prob_grad: float32 [2, 2048, 8], P('pp', 'cp')
- gate_grad: bfloat16 [2, 16, 1280, 3584], P('pp', 'cp', 'dp')
- up_grad: bfloat16 [2, 16, 1280, 3584], P('pp', 'cp', 'dp')
- down_grad: bfloat16 [2, 16, 1280, 3584], P('pp', 'cp', 'dp')
Inputs may be any that keep to these rules, and one draw needn't show every extreme that they name: `expert_ids`: in each aligned block of 128 tokens of a section, a token names 8 different experts, and no expert is named by more than 80 tokens of the block; some expert is named by exactly 80 tokens of some block.
All inputs are finite; a program needn't handle non-finite values.
Results may differ from a plain program's by a relative error of at most 0.012.
Values may be sent and summed in bfloat16 or wider, within the bound.
A program may use at most 128 MiB of HBM per device.

v0:
```python
import jax
import jax.numpy as jnp
from jax import lax
from jax.sharding import PartitionSpec as P


def passed_along(value, axis, steps):
    count = lax.axis_size(axis)
    leading, last = (max(0, -steps), min(count, count - steps))
    return lax.ppermute(value, axis, [(source, source + steps) for source in range(leading, last)])


def slot_table(block_ids, experts, capacity):
    flat_ids = block_ids.reshape(-1)
    one_hot = (flat_ids[:, None] == jnp.arange(experts, dtype=jnp.int32)[None, :]).astype(jnp.int32)
    before = jnp.cumsum(one_hot, axis=0) - one_hot
    slot_rank = jnp.sum(before * one_hot, axis=1)
    dest_index = flat_ids * capacity + slot_rank
    count = flat_ids.shape[0]
    anchor = (
        jnp.full((experts * capacity,), count, jnp.int32)
        .at[dest_index]
        .set(jnp.arange(count, dtype=jnp.int32))
    )
    return (dest_index, anchor)


def body(tokens, out_grad, probs, expert_ids, w_gate, w_up, w_down):
    tok_rows = tokens.shape[1]
    width = tokens.shape[2]
    top_count = probs.shape[2]
    experts = lax.axis_size("cp")
    replicas = lax.axis_size("dp")
    capacity = tok_rows * top_count * 5 // (4 * experts)
    dest_index, anchor = slot_table(expert_ids[0], experts, capacity)
    source_rows = anchor // top_count
    zero_row = jnp.zeros((1, width), jnp.bfloat16)
    sent_tokens = jnp.concatenate([tokens[0], zero_row], axis=0)[source_rows].reshape(
        experts, capacity, width
    )
    sent_grads = jnp.concatenate([out_grad[0], zero_row], axis=0)[source_rows].reshape(
        experts, capacity, width
    )
    sent_probs = jnp.concatenate([probs[0].reshape(-1), jnp.zeros((1,), jnp.bfloat16)])[
        anchor
    ].reshape(experts, capacity)
    got_tokens, got_grads, got_probs = (
        lax.all_to_all(sent_tokens, "cp", split_axis=0, concat_axis=0, tiled=True),
        lax.all_to_all(sent_grads, "cp", split_axis=0, concat_axis=0, tiled=True),
        lax.all_to_all(sent_probs, "cp", split_axis=0, concat_axis=0, tiled=True),
    )
    total_rows = experts * capacity
    rows_in = got_tokens.reshape(total_rows, width)
    grads_in = got_grads.reshape(total_rows, width)
    probs_in = got_probs.reshape(total_rows, 1).astype(jnp.float32)
    gate_mat = w_gate[0, 0]
    up_mat = w_up[0, 0]
    down_mat = w_down[0, 0]
    by_feature = (((1,), (1,)), ((), ()))
    by_row = (((0,), (0,)), ((), ()))
    gate_pre = lax.dot_general(rows_in, gate_mat, by_feature, preferred_element_type=jnp.float32)
    up_pre = lax.dot_general(rows_in, up_mat, by_feature, preferred_element_type=jnp.float32)
    grad_proj = lax.dot_general(grads_in, down_mat, by_feature, preferred_element_type=jnp.float32)
    sigma = jax.nn.sigmoid(gate_pre)
    silu_gate = gate_pre * sigma
    hidden = (silu_gate * up_pre).astype(jnp.bfloat16)
    prob_part = jnp.sum(hidden.astype(jnp.float32) * grad_proj, axis=1).astype(jnp.bfloat16)
    grad_hidden = probs_in * grad_proj
    grad_gate_pre = (grad_hidden * up_pre * sigma * (1.0 + gate_pre * (1.0 - sigma))).astype(
        jnp.bfloat16
    )
    grad_up_pre = (grad_hidden * silu_gate).astype(jnp.bfloat16)
    scaled_grad = (probs_in * grads_in).astype(jnp.bfloat16)
    input_part = jnp.dot(grad_gate_pre, gate_mat, preferred_element_type=jnp.float32)
    input_part = (
        input_part + jnp.dot(grad_up_pre, up_mat, preferred_element_type=jnp.float32)
    ).astype(jnp.bfloat16)
    gate_grad = lax.dot_general(
        grad_gate_pre, rows_in, by_row, preferred_element_type=jnp.float32
    ).astype(jnp.bfloat16)
    up_grad = lax.dot_general(
        grad_up_pre, rows_in, by_row, preferred_element_type=jnp.float32
    ).astype(jnp.bfloat16)
    down_grad = lax.dot_general(
        hidden, scaled_grad, by_row, preferred_element_type=jnp.float32
    ).astype(jnp.bfloat16)
    back_rows, back_probs = (
        lax.all_to_all(
            input_part.reshape(experts, capacity, width),
            "cp",
            split_axis=0,
            concat_axis=0,
            tiled=True,
        ),
        lax.all_to_all(
            prob_part.reshape(experts, capacity), "cp", split_axis=0, concat_axis=0, tiled=True
        ),
    )
    picked = back_rows.reshape(total_rows, width)[dest_index].reshape(tok_rows, top_count, width)
    input_sum = jnp.sum(picked.astype(jnp.float32), axis=1)
    prob_local = back_probs.reshape(-1)[dest_index].reshape(tok_rows, top_count).astype(jnp.float32)
    columns = width // replicas
    input_all, prob_all = lax.psum((input_sum, prob_local), "dp")
    own_columns = lax.dynamic_slice_in_dim(input_all, lax.axis_index("dp") * columns, columns, 1)
    passed = passed_along(own_columns.astype(jnp.bfloat16), "pp", -1)
    return (
        passed[None],
        prob_all[None],
        gate_grad[None, None],
        up_grad[None, None],
        down_grad[None, None],
    )


def solution(mesh):
    in_specs = (
        P("pp", "cp", None),
        P("pp", "cp", None),
        P("pp", "cp", None),
        P("pp", "cp", None),
        P("pp", "cp", "dp", None),
        P("pp", "cp", "dp", None),
        P("pp", "cp", "dp", None),
    )
    out_specs = (
        P("pp", "cp", "dp"),
        P("pp", "cp", None),
        P("pp", "cp", "dp", None),
        P("pp", "cp", "dp", None),
        P("pp", "cp", "dp", None),
    )
    return jax.shard_map(body, mesh=mesh, in_specs=in_specs, out_specs=out_specs, check_vma=False)
```

profile of v0, /device:TPU:1, one launch (start us, length us, event | category | flops | bytes accessed | tf_op | source)
XLA Modules:
  0.0 817.6 jit_solution(18104591402779993891)
XLA Ops:
  0.6 0.8 broadcast_multiply_fusion
  1.4 0.8 copy.23
  2.4 0.8 copy.21
  3.5 4.5 reduce-window.6
  8.5 4.3 scatter_custom_fusion
  12.9 8.0 gather_fusion
  21.6 10.0 %all-to-all-start = ((bf16[16,1,80]{2,1,0:T(2,128)(2,1)}), bf16[16,1,80]{2,1,0:T(2,128)(2,1)S(1)}, u32[]{:S(2)}, u32[]{:S(2)}) async-start(bf16[16,1,80]{2,1,0:T(2,128)(2,1)} %all_to_all.25), calls=%async_computation | async-start | bytes 16384 | tf_op jit(solution)/shard_map/all_to_all | solution.py:50
  31.6 1.2 concatenate.11
  32.9 7.9 gather_fusion.2
  40.8 7.7 all-to-all-start.2
  48.6 7.9 gather_fusion.1
  56.5 199.4 %all-to-all-done.2 = bf16[16,80,3584]{2,1,0:T(8,128)(2,1)} async-done(((bf16[16,80,3584]{2,1,0:T(8,128)(2,1)}), bf16[16,80,3584]{2,1,0:T(8,128)(2,1)}, u32[]{:S(2)}, u32[]{:S(2)}) %all-to-all-start.2) | async-done | bytes 9175072 | tf_op jit(solution)/shard_map/all_to_all | solution.py:48
  255.9 9.4 %all-to-all-start.1 = ((bf16[16,80,3584]{2,1,0:T(8,128)(2,1)}), bf16[16,80,3584]{2,1,0:T(8,128)(2,1)}, u32[]{:S(2)}, u32[]{:S(2)}) async-start(bf16[16,80,3584]{2,1,0:T(8,128)(2,1)} %bitcast.65), calls=%async_computation.1 | async-start | bytes 18350080 | tf_op jit(solution)/shard_map/all_to_all | solution.py:49
  265.4 7.7 fusion.9
  273.1 7.6 fusion.12
  280.7 192.8 %all-to-all-done.1 = bf16[16,80,3584]{2,1,0:T(8,128)(2,1)} async-done(((bf16[16,80,3584]{2,1,0:T(8,128)(2,1)}), bf16[16,80,3584]{2,1,0:T(8,128)(2,1)}, u32[]{:S(2)}, u32[]{:S(2)}) %all-to-all-start.1) | async-done | bytes 9175072 | tf_op jit(solution)/shard_map/all_to_all | solution.py:49
  473.5 8.4 %multiply_reduce_fusion = (bf16[1280]{0:T(1024)(128)(2,1)S(1)}, bf16[1280,160]{0,1:T(8,128)(2,1)}, bf16[1280,160]{0,1:T(8,128)(2,1)S(1)}, bf16[1280,160]{0,1:T(8,128)(2,1)S(1)}) fusion(f32[1280,160]{0,1:T(8,128)} %fusion.12, f32[1280,160]{0,1:T(8,128)} %fusion.9, f32[1280]{0:T(1024)S(1)} %reshape.121, bf16[1280,3584]{1,0:T(8,128)(2,1)} %bitcast.6, ...), kind=kOutput, calls=%fused_computation.27 | convolution fusion | flops 1471896320 | bytes 13196800 | tf_op jit(solution)/shard_map/dot_general | solution.py:63
  482.5 9.4 %all-to-all-start.4 = ((bf16[16,1,80]{2,1,0:T(2,128)(2,1)}), bf16[16,1,80]{2,1,0:T(2,128)(2,1)S(1)}, u32[]{:S(2)}, u32[]{:S(2)}) async-start(bf16[16,1,80]{2,1,0:T(2,128)(2,1)} %convert_element_type.101), calls=%async_computation.4 | async-start | bytes 16384 | tf_op jit(solution)/shard_map/all_to_all | solution.py:95
  491.9 8.9 %fusion.7 = f32[1280,3584]{1,0:T(8,128)} fusion(bf16[1280,160]{0,1:T(8,128)(2,1)S(1)} %get-tuple-element.19, bf16[1,1,160,3584]{3,2,1,0:T(8,128)(2,1)S(1)} %copy-done), kind=kOutput, calls=%fused_computation.18 | convolution fusion | flops 1468006400 | bytes 19906560 | tf_op jit(solution)/shard_map/dot_general | solution.py:74
  500.8 12.3 %fusion = bf16[1280,3584]{1,0:T(8,128)(2,1)} fusion(f32[1280,3584]{1,0:T(8,128)} %fusion.7, bf16[1280,160]{0,1:T(8,128)(2,1)S(1)} %get-tuple-element.20, bf16[1,1,160,3584]{3,2,1,0:T(8,128)(2,1)S(1)} %copy-done.1), kind=kOutput, calls=%fused_computation.8 | convolution fusion | flops 1477181440 | bytes 29081600 | tf_op jit(solution)/shard_map/dot_general | solution.py:76
  513.1 7.6 all-to-all-start.3
  520.7 6.3 fusion.5
  527.0 6.5 fusion.4
  533.6 6.8 gather_fusion.4
  540.5 188.0 %all-to-all-done.3 = bf16[16,80,3584]{2,1,0:T(8,128)(2,1)} async-done(((bf16[16,80,3584]{2,1,0:T(8,128)(2,1)}), bf16[16,80,3584]{2,1,0:T(8,128)(2,1)}, u32[]{:S(2)}, u32[]{:S(2)}) %all-to-all-start.3) | async-done | bytes 9175072 | tf_op jit(solution)/shard_map/all_to_all | solution.py:88
  728.5 18.6 %gather_fusion.3 = bf16[1024,3584]{1,0:T(8,128)(2,1)} fusion(bf16[1280,3584]{1,0:T(8,128)(2,1)} %bitcast.14, s32[1024]{0:T(1024)S(1)} %broadcast_clamp_fusion), kind=kCustom, calls=%fused_computation.3 | custom fusion | bytes 14684160 | tf_op jit(solution)/shard_map/gather | solution.py:99
  747.1 7.9 convert_reduce_fusion
  755.0 52.6 %all-reduce.4 = (bf16[128,3584]{1,0:T(8,128)(2,1)}, f32[1,128,8]{2,1,0:T(8,128)S(1)}) all-reduce(f32[128,3584]{1,0:T(8,128)S(1)} %convert_reduce_fusion, f32[1,128,8]{2,1,0:T(8,128)S(1)} %broadcast_in_dim.34), channel_id=1, replica_groups=mesh['pp'=2,'dp'=8,'cp'=16] {'dp'}, use_global_device_ids=true, to_apply=%region_5.6 | all-reduce | flops 459776 | bytes 2760704 | tf_op jit(solution)/shard_map/psum | solution.py:103
  807.6 1.0 dynamic-slice_convert_fusion
  808.6 1.3 collective-permute-start
  809.9 6.3 fusion.6
  816.8 0.8 copy.29
  (39 shorter events, 3.4 us)
Async XLA Ops:
  0.6 264.8 %copy-start = (bf16[1,1,160,3584]{3,2,1,0:T(8,128)(2,1)S(1)}, bf16[1,1,160,3584]{3,2,1,0:T(8,128)(2,1)}, u32[]{:S(2)}) copy-start(bf16[1,1,160,3584]{3,2,1,0:T(8,128)(2,1)} %param.11) | copy-start | bytes 3440644
  21.6 19.2 %all-to-all-start = ((bf16[16,1,80]{2,1,0:T(2,128)(2,1)}), bf16[16,1,80]{2,1,0:T(2,128)(2,1)S(1)}, u32[]{:S(2)}, u32[]{:S(2)}) async-start(bf16[16,1,80]{2,1,0:T(2,128)(2,1)} %all_to_all.25), calls=%async_computation | async-start | bytes 16384 | tf_op jit(solution)/shard_map/all_to_all | solution.py:50
  40.8 7.7 copy-start.2
  40.8 215.1 %all-to-all-start.2 = ((bf16[16,80,3584]{2,1,0:T(8,128)(2,1)}), bf16[16,80,3584]{2,1,0:T(8,128)(2,1)}, u32[]{:S(2)}, u32[]{:S(2)}) async-start(bf16[16,80,3584]{2,1,0:T(8,128)(2,1)} %bitcast.66), calls=%async_computation.2 | async-start | bytes 18350080 | tf_op jit(solution)/shard_map/all_to_all | solution.py:48
  255.9 217.6 %all-to-all-start.1 = ((bf16[16,80,3584]{2,1,0:T(8,128)(2,1)}), bf16[16,80,3584]{2,1,0:T(8,128)(2,1)}, u32[]{:S(2)}, u32[]{:S(2)}) async-start(bf16[16,80,3584]{2,1,0:T(8,128)(2,1)} %bitcast.65), calls=%async_computation.1 | async-start | bytes 18350080 | tf_op jit(solution)/shard_map/all_to_all | solution.py:49
  265.3 7.8 copy-start.1
  482.5 30.6 %all-to-all-start.4 = ((bf16[16,1,80]{2,1,0:T(2,128)(2,1)}), bf16[16,1,80]{2,1,0:T(2,128)(2,1)S(1)}, u32[]{:S(2)}, u32[]{:S(2)}) async-start(bf16[16,1,80]{2,1,0:T(2,128)(2,1)} %convert_element_type.101), calls=%async_computation.4 | async-start | bytes 16384 | tf_op jit(solution)/shard_map/all_to_all | solution.py:95
  513.1 215.4 %all-to-all-start.3 = ((bf16[16,80,3584]{2,1,0:T(8,128)(2,1)}), bf16[16,80,3584]{2,1,0:T(8,128)(2,1)}, u32[]{:S(2)}, u32[]{:S(2)}) async-start(bf16[16,80,3584]{2,1,0:T(8,128)(2,1)} %bitcast.64), calls=%async_computation.3 | async-start | bytes 18350080 | tf_op jit(solution)/shard_map/all_to_all | solution.py:88
  520.7 6.3 copy-start.3
  808.6 8.2 %collective-permute-start = (bf16[128,448]{1,0:T(8,128)(2,1)S(1)}, bf16[128,448]{1,0:T(8,128)(2,1)S(1)}, u32[]{:S(2)}, u32[]{:S(2)}) collective-permute-start(bf16[128,448]{1,0:T(8,128)(2,1)S(1)} %dynamic-slice_convert_fusion), channel_id=1, source_target_pairs={{128,0},{129,1},{130,2},{131,3},{132,4},{133,5},{134,6},{135,7},{1... | collective-permute-start | bytes 344072 | tf_op jit(solution)/shard_map/ppermute | solution.py:10
where the time goes:
time: 825 us; the launch traced here: 818 us
  waiting for transfers between devices  580 us (70%)
  matrix products  63.9 us (8%)
  local copies, waits for them, and re-layouts  61.2 us (7%)
  blocking collectives  52.6 us (6%)
  starting transfers between devices  45.5 us (6%)
  other arithmetic  13.5 us (2%)
    all_to_all x1, waiting for transfers between devices, body(): lax.all_to_all(sent_tokens, 'cp', split_axis=0, concat_axis=0, tiled=True)  199 us
    all_to_all x1, waiting for transfers between devices, body(): lax.all_to_all(sent_grads, 'cp', split_axis=0, concat_axis=0, tiled=True)  193 us
    all_to_all x1, waiting for transfers between devices, body(): lax.all_to_all(input_part.reshape(experts, capacity, width), 'cp', split_...  188 us
    psum x1, blocking collectives, body(): input_all, prob_all = lax.psum((input_sum, prob_local), 'dp')  52.6 us
    gather x1, local copies, waits for them, and re-layouts, body(): back_rows.reshape(total_rows, width)[dest_index]  18.6 us
  transfers between devices with their start and end apart: 6, of which 3 were waited for; matrix products, arithmetic and copies ran while one was open for 10% of the time, Pallas kernels for 0%

commit v1 on v0

v1 whole, which is shorter than its diff:
```python
import jax
import jax.numpy as jnp
from jax import lax
from jax.sharding import PartitionSpec as P

CAP_NUM, CAP_DEN = 5, 4


def body(tokens, out_grad, probs, expert_ids, w_gate, w_up, w_down):
    tok_rows = tokens.shape[1]
    width = tokens.shape[2]
    top_count = probs.shape[2]
    experts = lax.axis_size("cp")
    replicas = lax.axis_size("dp")
    capacity = tok_rows * top_count * CAP_NUM // (CAP_DEN * experts)
    columns = width // replicas
    dp = lax.axis_index("dp")
    me = lax.axis_index("cp")
    own = lax.dynamic_slice_in_dim(
        jnp.stack([tokens[0], out_grad[0]]), dp * columns, columns, 2
    )
    blocks = lax.all_gather(own, "cp")
    ids_all = lax.all_gather(expert_ids[0], "cp")
    probs_all = lax.all_gather(probs[0], "cp")
    match = ids_all == me
    has = jnp.any(match, axis=2)
    prob_tok = jnp.sum(jnp.where(match, probs_all.astype(jnp.float32), 0.0), axis=2)
    has_i = has.astype(jnp.int32)
    slot = jnp.cumsum(has_i, axis=1) - has_i
    pick = (slot[:, None, :] == jnp.arange(capacity)[None, :, None]) & has[:, None, :]
    probs_in = jnp.sum(jnp.where(pick, prob_tok[:, None, :], 0.0), axis=2).reshape(-1, 1)
    rows = jnp.einsum(
        "bct,bstd->sbcd", pick.astype(jnp.bfloat16), blocks, preferred_element_type=jnp.float32
    ).astype(jnp.bfloat16)
    total_rows = experts * capacity
    rows = rows.reshape(2 * total_rows, columns)
    full = lax.all_gather(rows, "dp", axis=1, tiled=True)
    rows_in, grads_in = full[:total_rows], full[total_rows:]
    gate_mat = w_gate[0, 0]
    up_mat = w_up[0, 0]
    down_mat = w_down[0, 0]
    by_feature = (((1,), (1,)), ((), ()))
    by_row = (((0,), (0,)), ((), ()))
    gate_pre = lax.dot_general(rows_in, gate_mat, by_feature, preferred_element_type=jnp.float32)
    up_pre = lax.dot_general(rows_in, up_mat, by_feature, preferred_element_type=jnp.float32)
    grad_proj = lax.dot_general(grads_in, down_mat, by_feature, preferred_element_type=jnp.float32)
    sigma = jax.nn.sigmoid(gate_pre)
    silu_gate = gate_pre * sigma
    hidden = (silu_gate * up_pre).astype(jnp.bfloat16)
    prob_part = jnp.sum(hidden.astype(jnp.float32) * grad_proj, axis=1)
    grad_hidden = probs_in * grad_proj
    grad_gate_pre = (grad_hidden * up_pre * sigma * (1.0 + gate_pre * (1.0 - sigma))).astype(
        jnp.bfloat16
    )
    grad_up_pre = (grad_hidden * silu_gate).astype(jnp.bfloat16)
    scaled_hidden = hidden
    scaled_grad = (probs_in * grads_in).astype(jnp.bfloat16)
    input_part = jnp.dot(grad_gate_pre, gate_mat, preferred_element_type=jnp.float32)
    input_part = (
        input_part + jnp.dot(grad_up_pre, up_mat, preferred_element_type=jnp.float32)
    ).astype(jnp.bfloat16)
    gate_grad = lax.dot_general(
        grad_gate_pre, rows_in, by_row, preferred_element_type=jnp.float32
    ).astype(jnp.bfloat16)
    up_grad = lax.dot_general(
        grad_up_pre, rows_in, by_row, preferred_element_type=jnp.float32
    ).astype(jnp.bfloat16)
    down_grad = lax.dot_general(
        scaled_hidden, scaled_grad, by_row, preferred_element_type=jnp.float32
    ).astype(jnp.bfloat16)
    reduced = lax.psum_scatter(input_part, "dp", scatter_dimension=1, tiled=True)
    back = lax.all_to_all(
        reduced.reshape(experts, capacity, columns), "cp", split_axis=0, concat_axis=0, tiled=True
    )
    back_probs = lax.all_to_all(
        prob_part.reshape(experts, capacity), "cp", split_axis=0, concat_axis=0, tiled=True
    )
    back_probs = lax.psum(back_probs, "dp")
    one_hot = expert_ids[0][:, :, None] == jnp.arange(experts)[None, None, :]
    has_e = jnp.any(one_hot, axis=1).astype(jnp.int32)
    slot_e = jnp.cumsum(has_e, axis=0) - has_e
    pick_e = (slot_e[:, :, None] == jnp.arange(capacity)[None, None, :]) & (has_e[:, :, None] > 0)
    input_sum = jnp.dot(
        pick_e.reshape(tok_rows, total_rows).astype(jnp.bfloat16),
        back.reshape(total_rows, columns),
        preferred_element_type=jnp.float32,
    )
    prob_te = jnp.sum(jnp.where(pick_e, back_probs[None], 0.0), axis=2)
    prob_grad = jnp.sum(jnp.where(one_hot, prob_te[:, None, :], 0.0), axis=2)
    passed = lax.ppermute(input_sum.astype(jnp.bfloat16), "pp", [(1, 0)])
    return (
        passed[None],
        prob_grad[None],
        gate_grad[None, None],
        up_grad[None, None],
        down_grad[None, None],
    )


def solution(mesh):
    in_specs = (
        P("pp", "cp", None),
        P("pp", "cp", None),
        P("pp", "cp", None),
        P("pp", "cp", None),
        P("pp", "cp", "dp", None),
        P("pp", "cp", "dp", None),
        P("pp", "cp", "dp", None),
    )
    out_specs = (
        P("pp", "cp", "dp"),
        P("pp", "cp", None),
        P("pp", "cp", "dp", None),
        P("pp", "cp", "dp", None),
        P("pp", "cp", "dp", None),
    )
    return jax.shard_map(body, mesh=mesh, in_specs=in_specs, out_specs=out_specs, check_vma=False)
```

time: 825 us -> 370 us (0.45)
  waiting for transfers between devices: 580 us -> 188 us
  local copies, waits for them, and re-layouts: 61.2 us -> 14 us
  starting transfers between devices: 45.5 us -> 17.1 us
  blocking collectives: 52.6 us -> 69.5 us
  between operations: 0.87 us -> 13.9 us
  other arithmetic: 13.5 us -> 2.56 us
    all_to_all x4 -> x1, waiting for transfers between devices: 580 us -> 0.01 us  [body(): lax.all_to_all(reduced.reshape(experts, capacity, columns), 'cp', split_a...]
    all_gather x0 -> x2, waiting for transfers between devices: none -> 133 us  [the longest x1 97 us: body(): full = lax.all_gather(rows, 'dp', axis=1, tiled=True)]
    all_gather x0 -> x2, blocking collectives: none -> 55.7 us  [the longest x1 30.6 us: body(): probs_all = lax.all_gather(probs[0], 'cp')]
    reduce_scatter x0 -> x1, waiting for transfers between devices: none -> 49.7 us  [body(): lax.psum_scatter(input_part, 'dp', scatter_dimension=1, tiled=True)]
    gather x5 -> x0, local copies, waits for them, and re-layouts: 49.1 us -> none  [the longest x1 18.6 us: body(): back_rows.reshape(total_rows, width)[dest_index]]
    psum x1, blocking collectives: 52.6 us -> 13.8 us  [body(): back_probs = lax.psum(back_probs, 'dp')]
    all_to_all x4 -> x1, starting transfers between devices: 34.8 us -> 7.75 us  [body(): lax.all_to_all(reduced.reshape(experts, capacity, columns), 'cp', split_a...]
  transfers between devices with their start and end apart: 6 -> 6, of which waited for: 3 -> 4; matrix products, arithmetic and copies ran while one was open for 10% -> 8% of each run, Pallas kernels for 0% -> 0%
where the time goes in v1:
time: 370 us; the launch traced here: 369 us
  waiting for transfers between devices  188 us (51%)
  blocking collectives  69.5 us (19%)
  matrix products  63.8 us (17%)
  starting transfers between devices  17.1 us (5%)
  local copies, waits for them, and re-layouts  14 us (4%)
  between operations  13.9 us (4%)
    all_gather x1, waiting for transfers between devices, body(): full = lax.all_gather(rows, 'dp', axis=1, tiled=True)  97 us
    reduce_scatter x1, waiting for transfers between devices, body(): lax.psum_scatter(input_part, 'dp', scatter_dimension=1, tiled=True)  49.7 us
    all_gather x1, waiting for transfers between devices, body(): blocks = lax.all_gather(own, 'cp')  36.2 us
    all_gather x1, blocking collectives, body(): probs_all = lax.all_gather(probs[0], 'cp')  30.6 us
    all_gather x1, blocking collectives, body(): ids_all = lax.all_gather(expert_ids[0], 'cp')  25.2 us
    psum x1, blocking collectives, body(): back_probs = lax.psum(back_probs, 'dp')  13.8 us
    dot_general x1, matrix products, body(): jnp.dot(grad_up_pre, up_mat, preferred_element_type=jnp.float32)  12.4 us
    dot_general x1, matrix products, body(): jnp.dot(grad_gate_pre, gate_mat, preferred_element_type=jnp.float32)  8.93 us
  transfers between devices with their start and end apart: 6, of which 4 were waited for; matrix products, arithmetic and copies ran while one was open for 8% of the time, Pallas kernels for 0%

profile of v1, /device:TPU:1, one launch (start us, length us, event | category | flops | bytes accessed | tf_op | source)
XLA Modules:
  0.0 368.9 jit_solution(6365457031545415939)
XLA Ops:
  7.3 1.6 copy.35
  8.9 1.6 copy.36
  10.5 0.7 fusion.45
  11.3 30.6 %all_gather.16 = bf16[16,128,8]{1,2,0:T(8,128)(2,1)S(1)} all-gather(bf16[1,128,8]{1,2,0:T(8,128)(2,1)S(1)} %copy-done.4), channel_id=1, replica_groups=mesh['pp'=2,'dp'=8,'cp'=16] {'cp'}, dimensions={0}, use_global_device_ids=true | all-gather | bytes 34816 | tf_op jit(solution)/shard_map/all_gather | solution.py:24
  41.8 25.2 %all_gather.15 = s32[16,128,8]{1,2,0:T(8,128)S(1)} all-gather(s32[1,128,8]{1,2,0:T(8,128)S(1)} %copy-done.3), channel_id=1, replica_groups=mesh['pp'=2,'dp'=8,'cp'=16] {'cp'}, dimensions={0}, use_global_device_ids=true | all-gather | bytes 69632 | tf_op jit(solution)/shard_map/all_gather | solution.py:23
  67.4 36.2 %all-gather.6.cloned.1.call-done = bf16[32,128,448]{1,2,0:T(8,128)(2,1)} async-done(((bf16[2,128,448]{1,2,0:T(8,128)(2,1)}), bf16[32,128,448]{1,2,0:T(8,128)(2,1)}) %all-gather.6.cloned.1.call-update) | async-done | bytes 3670032 | tf_op jit(solution)/shard_map/all_gather | solution.py:22
  103.6 3.7 convert_bitcast_fusion
  107.2 1.7 copy.37
  109.0 4.6 %copy.38 = bf16[2560,448]{0,1:T(8,128)(2,1)} copy(bf16[2560,448]{1,0:T(8,128)(2,1)} %bitcast.46) | data formatting | bytes 4587520 | tf_op jit(solution)/shard_map/reshape | solution.py:36
  113.8 0.4 select_reduce_fusion.1
  114.2 97.0 %all-gather.4.cloned.1.call-done = bf16[2560,3584]{0,1:T(8,128)(2,1)} async-done(((bf16[2560,448]{0,1:T(8,128)(2,1)}), bf16[2560,3584]{0,1:T(8,128)(2,1)}) %all-gather.4.cloned.1.call-update) | async-done | bytes 18350096 | tf_op jit(solution)/shard_map/all_gather | solution.py:37
  211.2 5.4 %fusion.10 = f32[1280,160]{0,1:T(8,128)S(1)} fusion(bf16[2560,3584]{0,1:T(8,128)(2,1)} %all-gather.4.cloned.1.call-done, bf16[1,1,160,3584]{3,2,1,0:T(8,128)(2,1)S(1)} %copy-done.2), kind=kOutput, calls=%fused_computation.12 | convolution fusion | flops 1468006400 | bytes 11141120 | tf_op jit(solution)/shard_map/dot_general | solution.py:45
  216.7 6.1 %fusion.12 = f32[1280,160]{0,1:T(8,128)S(1)} fusion(bf16[2560,3584]{0,1:T(8,128)(2,1)} %all-gather.4.cloned.1.call-done, bf16[1,1,160,3584]{3,2,1,0:T(8,128)(2,1)S(1)} %copy-done), kind=kOutput, calls=%fused_computation.14 | convolution fusion | flops 1468006400 | bytes 11141120 | tf_op jit(solution)/shard_map/dot_general | solution.py:44
  222.7 0.4 copy-done.6
  223.2 3.2 multiply_reduce_fusion
  226.3 8.9 %fusion.29 = f32[1280,3584]{0,1:T(8,128)} fusion(bf16[1280,160]{0,1:T(8,128)(2,1)S(1)} %get-tuple-element.9, bf16[1,1,160,3584]{3,2,1,0:T(8,128)(2,1)S(1)} %copy-done), kind=kOutput, calls=%fused_computation.27 | convolution fusion | flops 1468006400 | bytes 19906560 | tf_op jit(solution)/shard_map/dot_general | solution.py:58
  235.3 12.4 %fusion = bf16[1280,3584]{0,1:T(8,128)(2,1)} fusion(f32[1280,3584]{0,1:T(8,128)} %fusion.29, bf16[1280,160]{0,1:T(8,128)(2,1)S(1)} %get-tuple-element.10, bf16[1,1,160,3584]{3,2,1,0:T(8,128)(2,1)S(1)} %copy-done.2), kind=kOutput, calls=%fused_computation.2 | convolution fusion | flops 1477181440 | bytes 29081600 | tf_op jit(solution)/shard_map/dot_general | solution.py:60
  248.0 0.7 all_to_all.12
  248.7 7.7 %all-to-all-start.1 = ((f32[16,1,80]{2,1,0:T(1,128)}), f32[16,1,80]{2,1,0:T(1,128)S(1)}, u32[]{:S(2)}, u32[]{:S(2)}) async-start(f32[16,1,80]{2,1,0:T(1,128)} %all_to_all.12), calls=%async_computation.2 | async-start | bytes 16384 | tf_op jit(solution)/shard_map/all_to_all | solution.py:75
  256.6 49.7 %reduce-scatter.2.cloned.1.call-done = bf16[1280,448]{0,1:T(8,128)(2,1)} async-done(((bf16[1280,3584]{0,1:T(8,128)(2,1)}), bf16[1280,448]{0,1:T(8,128)(2,1)}) %reduce-scatter.2.cloned.1.call-update) | async-done | bytes 1146896 | tf_op jit(solution)/shard_map/reduce_scatter | solution.py:71
  306.2 2.4 copy.39
  308.6 7.7 %all-to-all-start = ((bf16[16,80,448]{2,1,0:T(8,128)(2,1)}), bf16[16,80,448]{2,1,0:T(8,128)(2,1)S(1)}, u32[]{:S(2)}, u32[]{:S(2)}) async-start(bf16[16,80,448]{2,1,0:T(8,128)(2,1)} %bitcast.9), calls=%async_computation.1 | async-start | bytes 2621440 | tf_op jit(solution)/shard_map/all_to_all | solution.py:72
  316.4 7.8 %fusion.25 = bf16[1,1,160,3584]{3,2,1,0:T(8,128)(2,1)} fusion(bf16[1280,160]{0,1:T(8,128)(2,1)S(1)} %get-tuple-element.9, bf16[2560,3584]{0,1:T(8,128)(2,1)} %all-gather.4.cloned.1.call-done), kind=kOutput, calls=%fused_computation.21 | convolution fusion | flops 1468579840 | bytes 10731520 | tf_op jit(solution)/shard_map/dot_general | solution.py:62
  324.2 7.8 %fusion.22 = bf16[1,1,160,3584]{3,2,1,0:T(8,128)(2,1)} fusion(bf16[1280,160]{0,1:T(8,128)(2,1)S(1)} %get-tuple-element.10, bf16[2560,3584]{0,1:T(8,128)(2,1)} %all-gather.4.cloned.1.call-done), kind=kOutput, calls=%fused_computation.20 | convolution fusion | flops 1468579840 | bytes 10731520 | tf_op jit(solution)/shard_map/dot_general | solution.py:65
  332.1 7.9 %fusion.21 = bf16[1,1,160,3584]{3,2,1,0:T(8,128)(2,1)} fusion(bf16[1280,160]{0,1:T(8,128)(2,1)S(1)} %copy-done.7, f32[1280]{0:T(1024)S(1)} %mul.45, bf16[2560,3584]{0,1:T(8,128)(2,1)} %all-gather.4.cloned.1.call-done), kind=kOutput, calls=%fused_computation.19 | convolution fusion | flops 1482342400 | bytes 10736640 | tf_op jit(solution)/shard_map/dot_general | solution.py:68
  340.0 13.8 %psum.7 = f32[16,80]{1,0:T(8,128)S(1)} all-reduce(f32[16,80]{1,0:T(8,128)S(1)} %bitcast.51), channel_id=1, replica_groups=mesh['pp'=2,'dp'=8,'cp'=16] {'dp'}, use_global_device_ids=true, to_apply=%region_8.9 | all-reduce | flops 1280 | bytes 10240 | tf_op jit(solution)/shard_map/psum | solution.py:78
  353.8 0.6 fusion.28
  354.4 1.3 collective-permute-start
  355.7 0.3 select_reduce_fusion
  356.0 0.6 select_reduce_fusion.2
  356.6 5.1 %collective-permute-done = bf16[128,448]{0,1:T(8,128)(2,1)S(1)} collective-permute-done((bf16[128,448]{0,1:T(8,128)(2,1)S(1)}, bf16[128,448]{0,1:T(8,128)(2,1)S(1)}, u32[]{:S(2)}, u32[]{:S(2)}) %collective-permute-start) | collective-permute-done | bytes 114720 | tf_op jit(solution)/shard_map/ppermute | solution.py:90
  361.8 0.6 copy.42
  (36 shorter events, 1.3 us)
Async XLA Ops:
  7.2 209.5 %copy-start = (bf16[1,1,160,3584]{3,2,1,0:T(8,128)(2,1)S(1)}, bf16[1,1,160,3584]{3,2,1,0:T(8,128)(2,1)}, u32[]{:S(2)}) copy-start(bf16[1,1,160,3584]{3,2,1,0:T(8,128)(2,1)} %param.11) | copy-start | bytes 3440644
  7.2 4.1 %copy-start.4 = (bf16[1,128,8]{1,2,0:T(8,128)(2,1)S(1)}, bf16[1,128,8]{1,2,0:T(8,128)(2,1)}, u32[]{:S(2)}) copy-start(bf16[1,128,8]{1,2,0:T(8,128)(2,1)} %param.9) | copy-start | bytes 6148
  7.2 34.6 %copy-start.3 = (s32[1,128,8]{1,2,0:T(8,128)S(1)}, s32[1,128,8]{1,2,0:T(8,128)}, u32[]{:S(2)}) copy-start(s32[1,128,8]{1,2,0:T(8,128)} %param.10) | copy-start | bytes 12292
  7.2 96.4 %all-gather.6.cloned.1.call-start = ((), (), s32[]{:S(2)}) async-start(), calls=%async_computation.5 | async-start | bytes 3899392 | tf_op jit(solution)/shard_map/all_gather | solution.py:22
  11.2 200.0 %all-gather.4.cloned.1.call-start = ((), (), s32[]{:S(2)}) async-start(), calls=%async_computation.3 | async-start | bytes 20643840 | tf_op jit(solution)/shard_map/all_gather | solution.py:37
  109.0 102.3 %copy-start.2 = (bf16[1,1,160,3584]{3,2,1,0:T(8,128)(2,1)S(1)}, bf16[1,1,160,3584]{3,2,1,0:T(8,128)(2,1)}, u32[]{:S(2)}) copy-start(bf16[1,1,160,3584]{3,2,1,0:T(8,128)(2,1)} %param.12) | copy-start | bytes 3440644
  113.6 192.7 %reduce-scatter.2.cloned.1.call-start = ((), (), s32[]{:S(2)}) async-start(), calls=%async_computation.4 | async-start | bytes 10321920 | tf_op jit(solution)/shard_map/reduce_scatter | solution.py:71
  211.2 11.5 %copy-start.5 = (bf16[2560,3584]{0,1:T(8,128)(2,1)S(1)}, bf16[2560,3584]{0,1:T(8,128)(2,1)}, u32[]{:S(2)}) copy-start(bf16[2560,3584]{0,1:T(8,128)(2,1)} %all-gather.4.cloned.1.call-done) | copy-start | bytes 55050244
  216.6 6.5 %copy-start.6 = (bf16[1,1,160,3584]{3,2,1,0:T(8,128)(2,1)S(1)}, bf16[1,1,160,3584]{3,2,1,0:T(8,128)(2,1)}, u32[]{:S(2)}) copy-start(bf16[1,1,160,3584]{3,2,1,0:T(8,128)(2,1)} %param.13) | copy-start | bytes 3440644
  248.7 60.0 %all-to-all-start.1 = ((f32[16,1,80]{2,1,0:T(1,128)}), f32[16,1,80]{2,1,0:T(1,128)S(1)}, u32[]{:S(2)}, u32[]{:S(2)}) async-start(f32[16,1,80]{2,1,0:T(1,128)} %all_to_all.12), calls=%async_computation.2 | async-start | bytes 16384 | tf_op jit(solution)/shard_map/all_to_all | solution.py:75
  308.6 45.1 %all-to-all-start = ((bf16[16,80,448]{2,1,0:T(8,128)(2,1)}), bf16[16,80,448]{2,1,0:T(8,128)(2,1)S(1)}, u32[]{:S(2)}, u32[]{:S(2)}) async-start(bf16[16,80,448]{2,1,0:T(8,128)(2,1)} %bitcast.9), calls=%async_computation.1 | async-start | bytes 2621440 | tf_op jit(solution)/shard_map/all_to_all | solution.py:72
  324.2 7.8 %copy-start.7 = (bf16[1280,160]{0,1:T(8,128)(2,1)S(1)}, bf16[1280,160]{0,1:T(8,128)(2,1)}, u32[]{:S(2)}) copy-start(bf16[1280,160]{0,1:T(8,128)(2,1)} %get-tuple-element.6) | copy-start | bytes 1228804
  332.1 30.3 %copy-start.1 = (bf16[1,1,160,3584]{3,2,1,0:T(8,128)(2,1)S(1)}, bf16[1,1,160,3584]{3,2,1,0:T(8,128)(2,1)}, u32[]{:S(2)}) copy-start(bf16[1,1,160,3584]{3,2,1,0:T(8,128)(2,1)} %param.11) | copy-start | bytes 3440644
  354.4 7.4 %collective-permute-start = (bf16[128,448]{0,1:T(8,128)(2,1)S(1)}, bf16[128,448]{0,1:T(8,128)(2,1)S(1)}, u32[]{:S(2)}, u32[]{:S(2)}) collective-permute-start(bf16[128,448]{0,1:T(8,128)(2,1)S(1)} %fusion.28), channel_id=1, source_target_pairs={{128,0},{129,1},{130,2},{131,3},{132,4},{133,5},{134,6},{135,7},{1... | collective-permute-start | bytes 344072 | tf_op jit(solution)/shard_map/ppermute | solution.py:90
Sparse Core Ops, SparseCore 0:
  11.3 92.1 all-gather.5
  113.7 97.4 all-gather.3
  247.8 58.4 reduce-scatter.1

commit v2 on v1

v2 whole, which is shorter than its diff:
```python
import functools
import jax
import jax.numpy as jnp
from jax import lax
from jax.experimental import pallas as pl
from jax.experimental.pallas import tpu as pltpu
from jax.sharding import PartitionSpec as P

CAP_NUM, CAP_DEN = 5, 4
MESH = pl.DeviceIdType.MESH
F32, BF16 = jnp.float32, jnp.bfloat16


def expert_kernel(
    dims, tok, grd, ids, prb, w_gate, w_up, w_down,
    ip_out, prob_out, gg_out, ug_out, dg_out,
    blk, stg, xs, wg, wu, wd, hid, ggp, gup, ipb, grb,
    loc, zr, xr, cr, yt, yg, cf, snd, osem,
):
    tok_rows, width, experts, cap, nz, ny = dims
    quarter = width // 4
    route = 16
    pay = 2 * tok_rows + route
    half_pay = tok_rows + route
    dp = lax.axis_index("dp")
    cp = lax.axis_index("cp")
    ndp, ncp = 2 * ny, 2 * nz
    z, xl = cp // 2, cp % 2
    y, core = dp // 2, dp % 2
    half = y % 2
    mine_q = pl.multiple_of((half * 2 + core) * quarter, 128)
    other_q = pl.multiple_of(((1 - half) * 2 + core) * quarter, 128)
    cp_x = z * 2 + (1 - xl)
    dp_c = y * 2 + (1 - core)
    z_up = ((z + 1) % nz) * 2 + xl
    z_dn = ((z + nz - 1) % nz) * 2 + xl
    y_up = ((y + 1) % ny) * 2 + core
    y_dn = ((y + ny - 1) % ny) * 2 + core

    barrier = pltpu.get_barrier_semaphore()
    for where in (
        {"cp": cp_x}, {"cp": z_up}, {"cp": z_dn}, {"dp": dp_c}, {"dp": y_up}, {"dp": y_dn},
    ):
        pl.semaphore_signal(barrier, inc=1, device_id=where, device_id_type=MESH)

    loads = [
        pltpu.make_async_copy(
            tok.at[:, pl.ds(mine_q, quarter)], blk.at[z, pl.ds(0, tok_rows), :], loc.at[0]
        ),
        pltpu.make_async_copy(
            grd.at[:, pl.ds(mine_q, quarter)], blk.at[z, pl.ds(half_pay, tok_rows), :], loc.at[1]
        ),
    ]
    weights = [
        pltpu.make_async_copy(w_gate, wg, loc.at[2]),
        pltpu.make_async_copy(w_up, wu, loc.at[3]),
        pltpu.make_async_copy(w_down, wd, loc.at[4]),
    ]
    for c in loads:
        c.start()
    for c in weights:
        c.start()

    e_iota = lax.broadcasted_iota(jnp.int32, (experts, tok_rows), 0)
    has = jnp.zeros((experts, tok_rows), F32)
    wgt = jnp.zeros((experts, tok_rows), F32)
    id_val = ids[...]
    prb_val = prb[...].astype(F32)
    for k in range(id_val.shape[0]):
        hit = id_val[k : k + 1, :] == e_iota
        has = jnp.where(hit, 1.0, has)
        wgt = jnp.where(hit, prb_val[k : k + 1, :], wgt)
    earlier = (
        lax.broadcasted_iota(jnp.int32, (tok_rows, tok_rows), 0)
        < lax.broadcasted_iota(jnp.int32, (tok_rows, tok_rows), 1)
    )
    slot = jnp.dot(
        has.astype(BF16), jnp.where(earlier, 1.0, 0.0).astype(BF16), preferred_element_type=F32
    )
    slot = jnp.where(has > 0.0, slot, -1.0)
    blk[z, tok_rows:half_pay, :] = jnp.zeros((route, quarter), BF16)
    blk[z, tok_rows:half_pay, 0:tok_rows] = slot.astype(BF16)
    blk[z, tok_rows:half_pay, tok_rows : 2 * tok_rows] = wgt.astype(BF16)
    for c in loads:
        c.wait()
    pl.semaphore_wait(barrier, 6)

    def remote(src, dst, s, r, where):
        return pltpu.make_async_remote_copy(
            src_ref=src, dst_ref=dst, send_sem=s, recv_sem=r, device_id=where, device_id_type=MESH
        )

    first, second = pl.ds(0, half_pay), pl.ds(half_pay, tok_rows)
    s_z, s_x, s_c, s_t, s_g, s_f = (snd.at[j] for j in range(6))

    def z_at(i):
        away = (i + 1) // 2
        return (z + nz + jnp.where(i % 2 == 1, -away, away)) % nz

    def block_rows(zz, kind):
        lane = jnp.where(kind == 0, xl, 1 - xl)
        return pl.multiple_of((zz * 2 + lane) * cap, 16)

    def x_copy(i):
        zz = z_at(i)
        dst = xs.at[:, pl.ds(pl.multiple_of((zz * 2 + xl) * cap, 16), cap), pl.ds(mine_q, quarter)]
        return remote(stg.at[i], dst, s_x, xr.at[i], {"cp": cp_x})

    def share(i, kind):
        unit = kind * nz + i
        rows = pl.ds(block_rows(z_at(i), kind), cap)
        cols = pl.ds(mine_q, quarter)
        piece = xs.at[:, rows, cols]
        top, low = xs.at[0, rows, cols], xs.at[1, rows, cols]
        return (
            remote(piece, piece, s_c, cr.at[unit], {"dp": dp_c}),
            remote(top, top, s_t, yt.at[unit], {"dp": y_up}),
            remote(low, low, s_g, yg.at[unit], {"dp": y_dn}),
        )

    def from_y(i, kind):
        unit = kind * nz + i
        rows = pl.ds(block_rows(z_at(i), kind), cap)
        cols = pl.ds(other_q, quarter)
        piece = xs.at[:, rows, cols]
        top, low = xs.at[0, rows, cols], xs.at[1, rows, cols]
        return (
            remote(top, top, s_t, yt.at[unit], {"dp": y_up}),
            remote(low, low, s_g, yg.at[unit], {"dp": y_dn}),
            remote(piece, piece, s_f, cf.at[unit], {"dp": dp_c}),
        )

    def forward(i, kind):
        got_t, got_g, fwd = from_y(i, kind)
        got_t.wait_recv()
        got_g.wait_recv()
        fwd.start()

    def stage_block(i):
        zz = z_at(i)
        whole = blk.at[zz]

        @pl.when((i >= 1) & (i <= 6))
        def _():
            remote(whole, whole, s_z, zr.at[i], {"cp": z_up}).wait_recv()

        @pl.when(i == 7)
        def _():
            a, b = blk.at[zz, first, :], blk.at[zz, second, :]
            remote(a, a, s_z, zr.at[7], {"cp": z_up}).wait_recv()
            remote(b, b, s_z, zr.at[8], {"cp": z_dn}).wait_recv()

        @pl.when((i == 0) | (i == 1) | (i == 3))
        def _():
            remote(whole, whole, s_z, zr.at[jnp.where(i == 0, 1, i + 2)], {"cp": z_up}).start()

        @pl.when((i == 0) | (i == 2) | (i == 4))
        def _():
            remote(whole, whole, s_z, zr.at[i + 2], {"cp": z_dn}).start()

        @pl.when(i == 5)
        def _():
            a = blk.at[zz, first, :]
            remote(a, a, s_z, zr.at[7], {"cp": z_up}).start()

        @pl.when(i == 6)
        def _():
            b = blk.at[zz, second, :]
            remote(b, b, s_z, zr.at[8], {"cp": z_dn}).start()

        table = blk[zz, tok_rows:half_pay, 0 : 2 * tok_rows].astype(F32)
        slots, probs = table[:, :tok_rows], table[:, tok_rows:]
        c_iota = lax.broadcasted_iota(jnp.int32, (cap, tok_rows), 0).astype(F32)
        plain, scaled = [], []
        for expert in (cp, cp_x):
            sel = e_iota == expert
            s_row = jnp.sum(jnp.where(sel, slots, 0.0), axis=0, keepdims=True)
            p_row = jnp.sum(jnp.where(sel, probs, 0.0), axis=0, keepdims=True)
            hit = c_iota == s_row
            plain.append(jnp.where(hit, 1.0, 0.0).astype(BF16))
            scaled.append(jnp.where(hit, p_row, 0.0).astype(BF16))
        rows = pl.ds(block_rows(zz, 0), cap)
        cols = pl.ds(mine_q, quarter)
        for part, lo, onehots in ((0, 0, plain), (1, half_pay, scaled)):
            data = blk[zz, lo : lo + tok_rows, :]
            both = jnp.dot(
                jnp.concatenate(onehots, axis=0), data, preferred_element_type=F32
            ).astype(BF16)
            xs[part, rows, cols] = both[:cap]
            stg[i, part] = both[cap:]
        x_copy(i).start()
        for c in share(i, 0):
            c.start()

    by_feature = (((1,), (1,)), ((), ()))
    by_row = (((0,), (0,)), ((), ()))
    pair = 2 * cap

    def out_copy(zz, j):
        rows = pl.ds(pl.multiple_of(zz * pair, 16), pair)
        return pltpu.make_async_copy(ipb.at[j], ip_out.at[rows, :], osem.at[j])

    def compute(i):
        zz = z_at(i)
        for kind in (0, 1):
            own, _, _ = share(i, kind)
            own.wait_recv()
            _, _, fwd = from_y(i, kind)
            fwd.wait_recv()
        rows = pl.ds(pl.multiple_of(zz * pair, 16), pair)
        x_rows = xs[0, rows, :]
        gate_pre = lax.dot_general(x_rows, wg[...], by_feature, preferred_element_type=F32)
        up_pre = lax.dot_general(x_rows, wu[...], by_feature, preferred_element_type=F32)
        g_hid = lax.dot_general(xs[1, rows, :], wd[...], by_feature, preferred_element_type=F32)
        sigma = jax.nn.sigmoid(gate_pre)
        silu = gate_pre * sigma
        hidden = (silu * up_pre).astype(BF16)
        hid[rows, :] = hidden
        prob_out[rows, :] = jnp.sum(hidden.astype(F32) * g_hid, axis=1, keepdims=True)
        g_gate = (g_hid * up_pre * sigma * (1.0 + gate_pre * (1.0 - sigma))).astype(BF16)
        g_up = (g_hid * silu).astype(BF16)
        ggp[rows, :] = g_gate
        gup[rows, :] = g_up
        j = i % 2

        @pl.when(i >= 2)
        def _():
            out_copy(zz, j).wait()

        step = 512
        for lo in range(0, width, step):
            part = jnp.dot(g_gate, wg[:, lo : lo + step], preferred_element_type=F32)
            part += jnp.dot(g_up, wu[:, lo : lo + step], preferred_element_type=F32)
            ipb[j, :, lo : lo + step] = part.astype(BF16)
        out_copy(zz, j).start()

    def step_fn(i, carry):
        @pl.when(i < nz)
        def _():
            stage_block(i)

        @pl.when((i >= 1) & (i < nz + 1))
        def _():
            x_copy(i - 1).wait_recv()
            for c in share(i - 1, 1):
                c.start()

        @pl.when((i >= 2) & (i < nz + 2))
        def _():
            forward(i - 2, 0)

        @pl.when((i >= 3) & (i < nz + 3))
        def _():
            forward(i - 3, 1)

        @pl.when(i == 4)
        def _():
            for c in weights:
                c.wait()

        @pl.when(i >= 4)
        def _():
            compute(i - 4)

        return carry

    lax.fori_loop(0, nz + 4, step_fn, 0)

    step = 512
    ff = grb.shape[1]

    def grads(t, carry):
        cols = pl.ds(pl.multiple_of(t * step, 128), step)
        x_cols = xs[0, :, cols]
        grb[0, :, cols] = lax.dot_general(
            ggp[...], x_cols, by_row, preferred_element_type=F32
        ).astype(BF16)
        grb[1, :, cols] = lax.dot_general(
            gup[...], x_cols, by_row, preferred_element_type=F32
        ).astype(BF16)
        grb[2, :, cols] = lax.dot_general(
            hid[...], xs[1, :, cols], by_row, preferred_element_type=F32
        ).astype(BF16)
        return carry

    lax.fori_loop(0, width // step, grads, 0)
    outs = [
        pltpu.make_async_copy(grb.at[j], o, loc.at[j]) for j, o in enumerate((gg_out, ug_out, dg_out))
    ]
    for c in outs:
        c.start()
    cols, ocols = pl.ds(mine_q, quarter), pl.ds(other_q, quarter)
    seven = blk.at[pl.ds(0, nz - 1)]
    remote(seven, seven, s_z, zr.at[0], {"cp": z_up}).wait_send()
    remote(stg, stg, s_x, zr.at[0], {"cp": cp_x}).wait_send()
    a = xs.at[:, :, cols]
    remote(a, a, s_c, zr.at[0], {"dp": dp_c}).wait_send()
    a = xs.at[0, :, cols]
    remote(a, a, s_t, zr.at[0], {"dp": y_up}).wait_send()
    a = xs.at[1, :, cols]
    remote(a, a, s_g, zr.at[0], {"dp": y_dn}).wait_send()
    a = xs.at[:, :, ocols]
    remote(a, a, s_f, zr.at[0], {"dp": dp_c}).wait_send()
    out_copy(z, 0).wait()
    out_copy(z, 1).wait()
    for c in outs:
        c.wait()


def expert_call(tokens, out_grad, ids_t, probs_t, w_gate, w_up, w_down):
    tok_rows, width = tokens.shape
    experts = lax.axis_size("cp")
    nz, ny = experts // 2, lax.axis_size("dp") // 2
    top = ids_t.shape[0]
    cap = tok_rows * top * CAP_NUM // (CAP_DEN * experts)
    ff = w_gate.shape[0]
    rows = experts * cap
    quarter = width // 4
    pay = 2 * tok_rows + 16
    anyspace = pl.BlockSpec(memory_space=pl.ANY)
    vmem = pl.BlockSpec(memory_space=pltpu.VMEM)
    wshape = jax.ShapeDtypeStruct((ff, width), BF16)
    dma = pltpu.SemaphoreType.DMA
    return pl.pallas_call(
        functools.partial(expert_kernel, (tok_rows, width, experts, cap, nz, ny)),
        out_shape=(
            jax.ShapeDtypeStruct((rows, width), BF16),
            jax.ShapeDtypeStruct((rows, 1), F32),
            wshape, wshape, wshape,
        ),
        in_specs=[anyspace, anyspace, vmem, vmem, anyspace, anyspace, anyspace],
        out_specs=(anyspace, vmem, anyspace, anyspace, anyspace),
        scratch_shapes=[
            pltpu.VMEM((nz, pay, quarter), BF16),
            pltpu.VMEM((nz, 2, cap, quarter), BF16),
            pltpu.VMEM((2, rows, width), BF16),
            pltpu.VMEM((ff, width), BF16),
            pltpu.VMEM((ff, width), BF16),
            pltpu.VMEM((ff, width), BF16),
            pltpu.VMEM((rows, ff), BF16),
            pltpu.VMEM((rows, ff), BF16),
            pltpu.VMEM((rows, ff), BF16),
            pltpu.VMEM((2, 2 * cap, width), BF16),
            pltpu.VMEM((3, ff, width), BF16),
            dma((5,)), dma((9,)), dma((nz,)), dma((2 * nz,)), dma((2 * nz,)), dma((2 * nz,)),
            dma((2 * nz,)), dma((6,)), dma((2,)),
        ],
        compiler_params=pltpu.CompilerParams(
            collective_id=0, has_side_effects=True, vmem_limit_bytes=60 * 1024 * 1024
        ),
        name="expert",
    )(tokens, out_grad, ids_t, probs_t, w_gate, w_up, w_down)


def body(tokens, out_grad, probs, expert_ids, w_gate, w_up, w_down):
    tok_rows = tokens.shape[1]
    width = tokens.shape[2]
    top_count = probs.shape[2]
    experts = lax.axis_size("cp")
    replicas = lax.axis_size("dp")
    capacity = tok_rows * top_count * CAP_NUM // (CAP_DEN * experts)
    columns = width // replicas
    total_rows = experts * capacity
    input_part, prob_part, gate_grad, up_grad, down_grad = expert_call(
        tokens[0], out_grad[0], expert_ids[0].T, probs[0].T, w_gate[0, 0], w_up[0, 0], w_down[0, 0]
    )
    reduced = lax.psum_scatter(input_part, "dp", scatter_dimension=1, tiled=True)
    back = lax.all_to_all(
        reduced.reshape(experts, capacity, columns), "cp", split_axis=0, concat_axis=0, tiled=True
    )
    back_probs = lax.all_to_all(
        prob_part.reshape(experts, capacity), "cp", split_axis=0, concat_axis=0, tiled=True
    )
    back_probs = lax.psum(back_probs, "dp")
    one_hot = expert_ids[0][:, :, None] == jnp.arange(experts)[None, None, :]
    has_e = jnp.any(one_hot, axis=1).astype(jnp.int32)
    slot_e = jnp.cumsum(has_e, axis=0) - has_e
    pick_e = (slot_e[:, :, None] == jnp.arange(capacity)[None, None, :]) & (has_e[:, :, None] > 0)
    input_sum = jnp.dot(
        pick_e.reshape(tok_rows, total_rows).astype(jnp.bfloat16),
        back.reshape(total_rows, columns),
        preferred_element_type=jnp.float32,
    )
    prob_te = jnp.sum(jnp.where(pick_e, back_probs[None], 0.0), axis=2)
    prob_grad = jnp.sum(jnp.where(one_hot, prob_te[:, None, :], 0.0), axis=2)
    prob_grad = prob_grad / probs[0].astype(F32)
    passed = lax.ppermute(input_sum.astype(jnp.bfloat16), "pp", [(1, 0)])
    return (
        passed[None],
        prob_grad[None],
        gate_grad[None, None],
        up_grad[None, None],
        down_grad[None, None],
    )


def solution(mesh):
    in_specs = (
        P("pp", "cp", None),
        P("pp", "cp", None),
        P("pp", "cp", None),
        P("pp", "cp", None),
        P("pp", "cp", "dp", None),
        P("pp", "cp", "dp", None),
        P("pp", "cp", "dp", None),
    )
    out_specs = (
        P("pp", "cp", "dp"),
        P("pp", "cp", None),
        P("pp", "cp", "dp", None),
        P("pp", "cp", "dp", None),
        P("pp", "cp", "dp", None),
    )
    return jax.shard_map(body, mesh=mesh, in_specs=in_specs, out_specs=out_specs, check_vma=False)
```

time: 370 us -> 225 us (0.61)
  the two profiles are of different devices: /device:TPU:1 before, /device:TPU:8 now
where the time goes in v2:
time: 225 us; the launch traced here: 224 us
  Pallas kernels  83 us (37%)
  waiting for transfers between devices  76.5 us (34%)
  local copies, waits for them, and re-layouts  22.2 us (10%)
  starting transfers between devices  14.1 us (6%)
  between operations  14.1 us (6%)
  blocking collectives  12.2 us (5%)
    pallas_call x1, Pallas kernels, expert_call(): pl.pallas_call(functools.partial(expert_kernel, (tok_rows, width, experts...  83 us
    unnamed x2, waiting for transfers between devices  48.5 us
    all_to_all x1, waiting for transfers between devices, body(): lax.all_to_all(reduced.reshape(experts, capacity, columns), 'cp', split_a...  21.7 us
    unnamed x18, local copies, waits for them, and re-layouts  21.2 us
    psum x1, blocking collectives, body(): back_probs = lax.psum(back_probs, 'dp')  12.2 us
    all_to_all x1, starting transfers between devices, body(): lax.all_to_all(reduced.reshape(experts, capacity, columns), 'cp', split_a...  8.41 us
    ppermute x1, waiting for transfers between devices, body(): passed = lax.ppermute(input_sum.astype(jnp.bfloat16), 'pp', [(1, 0)])  6.28 us
  transfers between devices with their start and end apart: 4, of which 3 were waited for; matrix products, arithmetic and copies ran while one was open for 2% of the time, Pallas kernels for 0%

profile of v2, /device:TPU:8, one launch (start us, length us, event | category | flops | bytes accessed | tf_op | source)
XLA Modules:
  0.0 224.1 jit_solution(15169421616511812718)
XLA Ops:
  7.2 0.0 reduce-scatter.4.cloned.1.call-start
  7.2 83.0 %expert.1 = (bf16[1280,3584]{1,0:T(8,128)(2,1)}, f32[1280,1]{1,0:T(8,128)}, bf16[160,3584]{1,0:T(8,128)(2,1)}, bf16[160,3584]{1,0:T(8,128)(2,1)}, bf16[160,3584]{1,0:T(8,128)(2,1)}) custom-call(bf16[128,3584]{1,0:T(8,128)(2,1)} %bitcast.35, bf16[128,3584]{1,0:T(8,128)(2,1)} %bitcast.36, s32[8,128]{1,0:T(8,128)} %bitcast.38, bf16[8,128]{1,0:T(8,128)(2,1)} %bitcast.42, ...), custom_call_target="tpu_custom_call" | custom-call | tf_op jit(solution)/shard_map/expert/pallas_call | solution.py:324
  90.3 12.7 %copy.27 = bf16[1280,3584]{0,1:T(8,128)(2,1)} copy(bf16[1280,3584]{1,0:T(8,128)(2,1)} %get-tuple-element.10) | data formatting | bytes 18350080
  103.0 0.0 reduce-scatter.4.cloned.1.call-update
  103.0 1.1 copy-done.3
  104.1 0.2 reduce
  104.3 0.7 all_to_all.12
  105.0 4.4 %all-to-all-start.1 = ((f32[16,1,80]{2,1,0:T(1,128)}), f32[16,1,80]{2,1,0:T(1,128)S(1)}, u32[]{:S(2)}, u32[]{:S(2)}) async-start(f32[16,1,80]{2,1,0:T(1,128)} %bitcast.12), calls=%async_computation.1 | async-start | bytes 16384 | tf_op jit(solution)/shard_map/all_to_all | solution.py:371
  109.4 48.5 %reduce-scatter.4.cloned.1.call-done = bf16[448,1280]{1,0:T(8,128)(2,1)} async-done(((bf16[3584,1280]{1,0:T(8,128)(2,1)}), bf16[448,1280]{1,0:T(8,128)(2,1)}) %reduce-scatter.4.cloned.1.call-update) | async-done | bytes 1146896
  157.9 2.4 %copy.28 = bf16[1280,448]{1,0:T(8,128)(2,1)} copy(bf16[1280,448]{0,1:T(8,128)(2,1)} %bitcast.31) | data formatting | bytes 2293760
  160.3 0.0 all-to-all-done.1
  160.3 8.4 %all-to-all-start = ((bf16[16,80,448]{2,1,0:T(8,128)(2,1)}), bf16[16,80,448]{2,1,0:T(8,128)(2,1)S(1)}, u32[]{:S(2)}, u32[]{:S(2)}) async-start(bf16[16,80,448]{2,1,0:T(8,128)(2,1)} %bitcast.9), calls=%async_computation | async-start | bytes 2621440 | tf_op jit(solution)/shard_map/all_to_all | solution.py:368
  168.7 0.0 copy-start.5
  168.7 0.0 copy-done.4
  168.7 0.1 copy.23
  168.9 0.2 reduce_window_sum.11
  169.1 0.1 copy.24
  169.1 0.1 copy.25
  169.2 12.2 %psum.7 = f32[16,80]{1,0:T(8,128)S(1)} all-reduce(f32[16,80]{1,0:T(8,128)S(1)} %bitcast.41), channel_id=1, replica_groups=mesh['pp'=2,'dp'=8,'cp'=16] {'dp'}, use_global_device_ids=true, to_apply=%region_3.0 | all-reduce | flops 1280 | bytes 10240 | tf_op jit(solution)/shard_map/psum | solution.py:374
  181.4 0.3 select_reduce_fusion
  181.7 21.7 %all-to-all-done = bf16[16,80,448]{2,1,0:T(8,128)(2,1)S(1)} async-done(((bf16[16,80,448]{2,1,0:T(8,128)(2,1)}), bf16[16,80,448]{2,1,0:T(8,128)(2,1)S(1)}, u32[]{:S(2)}, u32[]{:S(2)}) %all-to-all-start) | async-done | bytes 1146912 | tf_op jit(solution)/shard_map/all_to_all | solution.py:368
  203.4 0.6 fusion
  204.1 1.3 collective-permute-start
  205.4 0.0 copy-done.5
  205.4 0.6 bitcast_divide_fusion
  206.0 6.3 %collective-permute-done = bf16[128,448]{0,1:T(8,128)(2,1)S(1)} collective-permute-done((bf16[128,448]{0,1:T(8,128)(2,1)S(1)}, bf16[128,448]{0,1:T(8,128)(2,1)S(1)}, u32[]{:S(2)}, u32[]{:S(2)}) %collective-permute-start) | collective-permute-done | bytes 114720 | tf_op jit(solution)/shard_map/ppermute | solution.py:387
  212.3 0.6 copy.33
  212.9 1.0 copy.34
  213.9 0.7 copy-done.1
  214.6 1.0 copy.35
  215.6 0.7 copy-done
  216.3 1.0 copy.36
  (10 shorter events, 0.1 us)
Async XLA Ops:
  7.2 150.7 %reduce-scatter.4.cloned.1.call-start = ((), (), s32[]{:S(2)}) async-start(), calls=%async_computation.3 | async-start | bytes 10321920
  103.0 1.1 copy-start.3
  105.0 55.3 %all-to-all-start.1 = ((f32[16,1,80]{2,1,0:T(1,128)}), f32[16,1,80]{2,1,0:T(1,128)S(1)}, u32[]{:S(2)}, u32[]{:S(2)}) async-start(f32[16,1,80]{2,1,0:T(1,128)} %bitcast.12), calls=%async_computation.1 | async-start | bytes 16384 | tf_op jit(solution)/shard_map/all_to_all | solution.py:371
  160.3 8.4 %copy-start.4 = (s32[1,128,8]{1,2,0:T(8,128)S(1)}, s32[1,128,8]{1,2,0:T(8,128)}, u32[]{:S(2)}) copy-start(s32[1,128,8]{1,2,0:T(8,128)} %param.10) | copy-start | bytes 12292
  160.3 43.2 %all-to-all-start = ((bf16[16,80,448]{2,1,0:T(8,128)(2,1)}), bf16[16,80,448]{2,1,0:T(8,128)(2,1)S(1)}, u32[]{:S(2)}, u32[]{:S(2)}) async-start(bf16[16,80,448]{2,1,0:T(8,128)(2,1)} %bitcast.9), calls=%async_computation | async-start | bytes 2621440 | tf_op jit(solution)/shard_map/all_to_all | solution.py:368
  168.7 36.7 %copy-start.5 = (bf16[1,128,8]{1,2,0:T(8,128)(2,1)S(1)}, bf16[1,128,8]{1,2,0:T(8,128)(2,1)}, u32[]{:S(2)}) copy-start(bf16[1,128,8]{1,2,0:T(8,128)(2,1)} %param.9) | copy-start | bytes 6148
  168.9 44.1 %copy-start.2 = (bf16[160,3584]{1,0:T(8,128)(2,1)S(1)}, bf16[160,3584]{1,0:T(8,128)(2,1)}, u32[]{:S(2)}) copy-start(bf16[160,3584]{1,0:T(8,128)(2,1)} %get-tuple-element.12) | copy-start | bytes 3440644
  204.1 8.2 %collective-permute-start = (bf16[128,448]{0,1:T(8,128)(2,1)S(1)}, bf16[128,448]{0,1:T(8,128)(2,1)S(1)}, u32[]{:S(2)}, u32[]{:S(2)}) collective-permute-start(bf16[128,448]{0,1:T(8,128)(2,1)S(1)} %fusion), channel_id=1, source_target_pairs={{128,0},{129,1},{130,2},{131,3},{132,4},{133,5},{134,6},{135,7},{1... | collective-permute-start | bytes 344072 | tf_op jit(solution)/shard_map/ppermute | solution.py:387
  212.9 1.7 copy-start.1
  214.6 1.7 copy-start
Sparse Core Ops, SparseCore 0:
  103.2 54.6 reduce-scatter.3

commit v3 on v2

--- a/solution.py
+++ b/solution.py
@@ -13,9 +13,10 @@
 
 def expert_kernel(
     dims, tok, grd, ids, prb, w_gate, w_up, w_down,
-    ip_out, prob_out, gg_out, ug_out, dg_out,
-    blk, stg, xs, wg, wu, wd, hid, ggp, gup, ipb, grb,
-    loc, zr, xr, cr, yt, yg, cf, snd, osem,
+    passed_out, prob_out, gg_out, ug_out, dg_out,
+    blk, stg, xs, wg, wu, wd, hid, ggp, gup, grb, ipb, c1r, farr, comr, dirr, l3r,
+    ptab, prcv, pcol, pfin, fxs, fxr, fin, zero,
+    loc, zr, xr, cr, yt, yg, cf, snd, c1m, fam, com, dim, l3m, ppm, pcm, psn, one,
 ):
     tok_rows, width, experts, cap, nz, ny = dims
     quarter = width // 4
@@ -37,11 +38,26 @@
     y_up = ((y + 1) % ny) * 2 + core
     y_dn = ((y + ny - 1) % ny) * 2 + core
 
+    pp = lax.axis_index("pp")
+    returns = pp == 1
+    same = core == xl
+    owner_dp = y * 2 + xl
+
+    def owner(zz):
+        return {"cp": zz * 2 + core, "dp": owner_dp}
+
     barrier = pltpu.get_barrier_semaphore()
     for where in (
         {"cp": cp_x}, {"cp": z_up}, {"cp": z_dn}, {"dp": dp_c}, {"dp": y_up}, {"dp": y_dn},
+        {"pp": 1 - pp},
     ):
         pl.semaphore_signal(barrier, inc=1, device_id=where, device_id_type=MESH)
+    for dz in range(1, nz):
+        pl.semaphore_signal(barrier, inc=1, device_id=owner((z + dz) % nz), device_id_type=MESH)
+
+    @pl.when(jnp.logical_not(same))
+    def _():
+        pl.semaphore_signal(barrier, inc=1, device_id=owner(z), device_id_type=MESH)
 
     loads = [
         pltpu.make_async_copy(
@@ -83,7 +99,9 @@
     blk[z, tok_rows:half_pay, tok_rows : 2 * tok_rows] = wgt.astype(BF16)
     for c in loads:
         c.wait()
-    pl.semaphore_wait(barrier, 6)
+    ptab[...] = jnp.zeros_like(ptab)
+    zero[...] = jnp.zeros_like(zero)
+    pl.semaphore_wait(barrier, 7 + nz - 1 + jnp.where(same, 0, 1))
 
     def remote(src, dst, s, r, where):
         return pltpu.make_async_remote_copy(
@@ -196,9 +214,69 @@
     by_row = (((0,), (0,)), ((), ()))
     pair = 2 * cap
 
-    def out_copy(zz, j):
-        rows = pl.ds(pl.multiple_of(zz * pair, 16), pair)
-        return pltpu.make_async_copy(ipb.at[j], ip_out.at[rows, :], osem.at[j])
+    chunk = width // ny
+    half_w = chunk // 2
+
+    def ccols(yy):
+        return pl.ds(pl.multiple_of(yy * chunk, 128), chunk)
+
+    def mine_of(i):
+        return ipb.at[i, pl.ds(pl.multiple_of(core * cap, 16), cap)]
+
+    def core_sum(i):
+        src = ipb.at[i, pl.ds(pl.multiple_of((1 - core) * cap, 16), cap)]
+        return remote(src, c1r.at[i], snd.at[6], c1m.at[i], {"dp": dp_c})
+
+    def y_steps(i):
+        up = i % 2 == 0
+        fwd_y = jnp.where(up, (y + 1) % ny, (y + ny - 1) % ny)
+        bwd_y = jnp.where(up, (y + ny - 1) % ny, (y + 1) % ny)
+        fwd_to, bwd_to = {"dp": fwd_y * 2 + core}, {"dp": bwd_y * 2 + core}
+        rows = pl.ds(pl.multiple_of(core * cap, 16), cap)
+        s_y = snd.at[7]
+        far = remote(
+            ipb.at[i, rows, ccols((y + 2) % ny)], farr.at[i], s_y, fam.at[i], fwd_to
+        )
+        comb = remote(ipb.at[i, rows, ccols(fwd_y)], comr.at[i], s_y, com.at[i], fwd_to)
+        direct = remote(ipb.at[i, rows, ccols(bwd_y)], dirr.at[i], s_y, dim.at[i], bwd_to)
+        return far, comb, direct, fwd_y, rows
+
+    def owner_copy(i):
+        rows = pl.ds(pl.multiple_of(core * cap, 16), cap)
+        return remote(
+            ipb.at[i, rows, ccols(y)], l3r.at[z], snd.at[8], l3m.at[z], owner(z_at(i))
+        )
+
+    def ret_a(i):
+        core_sum(i).wait_recv()
+        rows = pl.ds(pl.multiple_of(core * cap, 16), cap)
+        ipb[i, rows, :] = (ipb[i, rows, :].astype(F32) + c1r[i].astype(F32)).astype(BF16)
+        far, _, direct, _, _ = y_steps(i)
+        far.start()
+        direct.start()
+
+    def ret_b(i):
+        far, comb, _, fwd_y, rows = y_steps(i)
+        far.wait_recv()
+        cols = ccols(fwd_y)
+        ipb[i, rows, cols] = (ipb[i, rows, cols].astype(F32) + farr[i].astype(F32)).astype(BF16)
+        comb.start()
+
+    def ret_c(i):
+        _, comb, direct, _, rows = y_steps(i)
+        comb.wait_recv()
+        direct.wait_recv()
+        total = ipb[i, rows, ccols(y)].astype(F32) + comr[i].astype(F32) + dirr[i].astype(F32)
+        here = same & (i == 0)
+
+        @pl.when(here)
+        def _():
+            l3r[z] = total.astype(BF16)
+
+        @pl.when(jnp.logical_not(here))
+        def _():
+            ipb[i, rows, ccols(y)] = total.astype(BF16)
+            owner_copy(i).start()
 
     def compute(i):
         zz = z_at(i)
@@ -216,61 +294,91 @@
         silu = gate_pre * sigma
         hidden = (silu * up_pre).astype(BF16)
         hid[rows, :] = hidden
-        prob_out[rows, :] = jnp.sum(hidden.astype(F32) * g_hid, axis=1, keepdims=True)
+        prod = hidden.astype(F32) * g_hid
+        high = prod.astype(BF16)
+        low = (prod - high.astype(F32)).astype(BF16)
+        ones = jnp.ones((8, prod.shape[1]), BF16)
+        for k in (0, 1):
+            part = slice(k * cap, (k + 1) * cap)
+            sums = lax.dot_general(ones, high[part], by_feature, preferred_element_type=F32)
+            sums += lax.dot_general(ones, low[part], by_feature, preferred_element_type=F32)
+            ptab[0, zz * 2 + k, :, 0:cap] = sums
         g_gate = (g_hid * up_pre * sigma * (1.0 + gate_pre * (1.0 - sigma))).astype(BF16)
         g_up = (g_hid * silu).astype(BF16)
         ggp[rows, :] = g_gate
         gup[rows, :] = g_up
-        j = i % 2
-
-        @pl.when(i >= 2)
-        def _():
-            out_copy(zz, j).wait()
-
-        step = 512
-        for lo in range(0, width, step):
-            part = jnp.dot(g_gate, wg[:, lo : lo + step], preferred_element_type=F32)
-            part += jnp.dot(g_up, wu[:, lo : lo + step], preferred_element_type=F32)
-            ipb[j, :, lo : lo + step] = part.astype(BF16)
-        out_copy(zz, j).start()
-
-    def step_fn(i, carry):
-        @pl.when(i < nz)
-        def _():
-            stage_block(i)
-
-        @pl.when((i >= 1) & (i < nz + 1))
-        def _():
-            x_copy(i - 1).wait_recv()
-            for c in share(i - 1, 1):
-                c.start()
-
-        @pl.when((i >= 2) & (i < nz + 2))
-        def _():
-            forward(i - 2, 0)
-
-        @pl.when((i >= 3) & (i < nz + 3))
-        def _():
-            forward(i - 3, 1)
-
-        @pl.when(i == 4)
-        def _():
-            for c in weights:
-                c.wait()
-
-        @pl.when(i >= 4)
-        def _():
-            compute(i - 4)
-
-        return carry
-
-    lax.fori_loop(0, nz + 4, step_fn, 0)
-
-    step = 512
-    ff = grb.shape[1]
-
-    def grads(t, carry):
-        cols = pl.ds(pl.multiple_of(t * step, 128), step)
+
+        @pl.when(returns)
+        def _():
+            step = 512
+            for lo in range(0, width, step):
+                part = jnp.dot(g_gate, wg[:, lo : lo + step], preferred_element_type=F32)
+                part += jnp.dot(g_up, wu[:, lo : lo + step], preferred_element_type=F32)
+                ipb[i, :, lo : lo + step] = part.astype(BF16)
+            core_sum(i).start()
+
+    def pair_copy(r):
+        to = (dp_c, (y + 1 - 2 * (y % 2)) * 2 + core, (ny - 1 - y) * 2 + core)[r]
+        return remote(ptab.at[r], prcv.at[r], psn.at[r], ppm.at[r], {"dp": to})
+
+    def pair_sum(r):
+        pair_copy(r).wait_recv()
+        ptab[r + 1] = ptab[r] + prcv[r]
+
+    def prob_copy(dz):
+        zz = (z + dz) % nz
+        return remote(
+            ptab.at[3, zz * 2 + core], pcol.at[z], psn.at[3], pcm.at[z], owner(zz)
+        )
+
+    def prob_spread():
+        for dz in range(1, nz):
+            prob_copy(dz).start()
+
+        @pl.when(jnp.logical_not(same))
+        def _():
+            prob_copy(0).start()
+
+        @pl.when(same)
+        def _():
+            pcol[z] = ptab[3, z * 2 + core]
+
+    def own_hits(zz):
+        table = blk[z, tok_rows:half_pay, 0:tok_rows].astype(F32)
+        row = jnp.sum(jnp.where(e_iota == zz * 2 + core, table, 0.0), axis=0, keepdims=True)
+        c_iota = lax.broadcasted_iota(jnp.int32, (cap, tok_rows), 0).astype(F32)
+        return jnp.where(c_iota == row, 1.0, 0.0).astype(BF16)
+
+    def each_source(ref, sems, sem):
+        for dz in range(1, nz):
+            src = (z + dz) % nz
+            remote(ref.at[src], ref.at[src], sem, sems.at[src], owner(z)).wait_recv()
+
+        @pl.when(jnp.logical_not(same))
+        def _():
+            remote(ref.at[z], ref.at[z], sem, sems.at[z], owner(z)).wait_recv()
+
+    last_copy = remote(pfin.at[0], pfin.at[1], psn.at[4], one.at[0], {"dp": dp_c})
+
+    def prob_pick():
+        each_source(pcol, pcm, psn.at[3])
+        acc = jnp.zeros(id_val.shape, F32)
+        for zz in range(nz):
+            val = pcol[zz][:, 0:cap]
+            high = val.astype(BF16)
+            low = (val - high.astype(F32)).astype(BF16)
+            hits = own_hits(zz)
+            got = jnp.dot(high, hits, preferred_element_type=F32)
+            got += jnp.dot(low, hits, preferred_element_type=F32)
+            acc = jnp.where(ids[...] == zz * 2 + core, got, acc)
+        pfin[0] = acc
+        last_copy.start()
+
+    grad_step = 512
+    n_grad = width // grad_step
+
+    def grads(t):
+        cols = pl.ds(pl.multiple_of(t * grad_step, 128), grad_step)
         x_cols = xs[0, :, cols]
         grb[0, :, cols] = lax.dot_general(
             ggp[...], x_cols, by_row, preferred_element_type=F32
@@ -281,14 +389,104 @@
         grb[2, :, cols] = lax.dot_general(
             hid[...], xs[1, :, cols], by_row, preferred_element_type=F32
         ).astype(BF16)
+
+    def step_fn(i, carry):
+        @pl.when(i < nz)
+        def _():
+            stage_block(i)
+
+        @pl.when((i >= 1) & (i < nz + 1))
+        def _():
+            x_copy(i - 1).wait_recv()
+            for c in share(i - 1, 1):
+                c.start()
+
+        @pl.when((i >= 2) & (i < nz + 2))
+        def _():
+            forward(i - 2, 0)
+
+        @pl.when((i >= 3) & (i < nz + 3))
+        def _():
+            forward(i - 3, 1)
+
+        @pl.when(i == 4)
+        def _():
+            for c in weights:
+                c.wait()
+
+        for lag, stage in ((9, ret_c), (7, ret_b), (5, ret_a)):
+
+            @pl.when(returns & (i >= lag) & (i < nz + lag))
+            def _(lag=lag, stage=stage):
+                stage(i - lag)
+
+        @pl.when((i >= 4) & (i < nz + 4))
+        def _():
+            compute(i - 4)
+
+        first_free = nz + 4
+
+        @pl.when(i == first_free)
+        def _():
+            pair_copy(0).start()
+
+        for r in (0, 1):
+
+            @pl.when(i == first_free + 1 + r)
+            def _(r=r):
+                pair_sum(r)
+                pair_copy(r + 1).start()
+
+        @pl.when(i == first_free + 3)
+        def _():
+            pair_sum(2)
+            prob_spread()
+
+        @pl.when(i == first_free + 5)
+        def _():
+            prob_pick()
+
+        @pl.when(i >= first_free)
+        def _():
+            grads(i - first_free)
+
         return carry
 
-    lax.fori_loop(0, width // step, grads, 0)
+    lax.fori_loop(0, nz + 4 + n_grad, step_fn, 0)
+
     outs = [
         pltpu.make_async_copy(grb.at[j], o, loc.at[j]) for j, o in enumerate((gg_out, ug_out, dg_out))
     ]
     for c in outs:
         c.start()
+    hand_over = remote(fin, passed_out, snd.at[9], one.at[1], {"pp": 0})
+    swap = remote(fxs, fxr, snd.at[10], one.at[2], {"dp": dp_c})
+    blank = pltpu.make_async_copy(zero, passed_out, loc.at[3])
+
+    @pl.when(returns)
+    def _():
+        blank.start()
+        each_source(l3r, l3m, snd.at[8])
+        hits = jnp.concatenate([own_hits(zz) for zz in range(nz)], axis=0)
+        rows = jnp.concatenate([l3r[zz] for zz in range(nz)], axis=0)
+        tot = lax.dot_general(hits, rows, by_row, preferred_element_type=F32).T
+
+        @pl.when(core == 0)
+        def _():
+            fxs[...] = tot[half_w:]
+
+        @pl.when(core == 1)
+        def _():
+            fxs[...] = tot[:half_w]
+
+        swap.start()
+        kept = jnp.where(core == 0, tot[:half_w], tot[half_w:])
+        swap.wait_recv()
+        fin[...] = (kept + fxr[...]).astype(BF16)
+        hand_over.start()
+
+    last_copy.wait_recv()
+    prob_out[...] = (pfin[0] + pfin[1]) / prb[...].astype(F32)
     cols, ocols = pl.ds(mine_q, quarter), pl.ds(other_q, quarter)
     seven = blk.at[pl.ds(0, nz - 1)]
     remote(seven, seven, s_z, zr.at[0], {"cp": z_up}).wait_send()
@@ -301,8 +499,43 @@
     remote(a, a, s_g, zr.at[0], {"dp": y_dn}).wait_send()
     a = xs.at[:, :, ocols]
     remote(a, a, s_f, zr.at[0], {"dp": dp_c}).wait_send()
-    out_copy(z, 0).wait()
-    out_copy(z, 1).wait()
+    for r in (0, 1, 2):
+        pair_copy(r).wait_send()
+    last_copy.wait_send()
+    seven_p = pcol.at[pl.ds(0, nz - 1)]
+
+    @pl.when(same)
+    def _():
+        remote(seven_p, seven_p, psn.at[3], one.at[0], owner(z)).wait_send()
+
+    @pl.when(jnp.logical_not(same))
+    def _():
+        remote(pcol, pcol, psn.at[3], one.at[0], owner(z)).wait_send()
+
+    @pl.when(returns)
+    def _():
+        remote(c1r, c1r, snd.at[6], one.at[0], {"dp": dp_c}).wait_send()
+        total = farr.shape[0] * 3 * chunk // (2 * width)
+        sent = ipb.at[pl.ds(0, total)]
+        remote(sent, sent, snd.at[7], one.at[0], {"dp": y_up}).wait_send()
+        swap.wait_send()
+        hand_over.wait_send()
+        blank.wait()
+
+    seven_l = l3r.at[pl.ds(0, nz - 1)]
+
+    @pl.when(returns & same)
+    def _():
+        remote(seven_l, seven_l, snd.at[8], one.at[0], owner(z)).wait_send()
+
+    @pl.when(returns & jnp.logical_not(same))
+    def _():
+        remote(l3r, l3r, snd.at[8], one.at[0], owner(z)).wait_send()
+
+    @pl.when(jnp.logical_not(returns))
+    def _():
+        hand_over.wait_recv()
+
     for c in outs:
         c.wait()
 
@@ -324,8 +557,8 @@
     return pl.pallas_call(
         functools.partial(expert_kernel, (tok_rows, width, experts, cap, nz, ny)),
         out_shape=(
-            jax.ShapeDtypeStruct((rows, width), BF16),
-            jax.ShapeDtypeStruct((rows, 1), F32),
+            jax.ShapeDtypeStruct((width // (2 * ny), tok_rows), BF16),
+            jax.ShapeDtypeStruct((top, tok_rows), F32),
             wshape, wshape, wshape,
         ),
         in_specs=[anyspace, anyspace, vmem, vmem, anyspace, anyspace, anyspace],
@@ -340,10 +573,24 @@
             pltpu.VMEM((rows, ff), BF16),
             pltpu.VMEM((rows, ff), BF16),
             pltpu.VMEM((rows, ff), BF16),
-            pltpu.VMEM((2, 2 * cap, width), BF16),
             pltpu.VMEM((3, ff, width), BF16),
+            pltpu.VMEM((nz, 2 * cap, width), BF16),
+            pltpu.VMEM((nz, cap, width), BF16),
+            pltpu.VMEM((nz, cap, width // ny), BF16),
+            pltpu.VMEM((nz, cap, width // ny), BF16),
+            pltpu.VMEM((nz, cap, width // ny), BF16),
+            pltpu.VMEM((nz, cap, width // ny), BF16),
+            pltpu.VMEM((4, experts, 8, 128), F32),
+            pltpu.VMEM((3, experts, 8, 128), F32),
+            pltpu.VMEM((nz, 8, 128), F32),
+            pltpu.VMEM((2, top, tok_rows), F32),
+            pltpu.VMEM((width // (2 * ny), tok_rows), F32),
+            pltpu.VMEM((width // (2 * ny), tok_rows), F32),
+            pltpu.VMEM((width // (2 * ny), tok_rows), BF16),
+            pltpu.VMEM((width // (2 * ny), tok_rows), BF16),
             dma((5,)), dma((9,)), dma((nz,)), dma((2 * nz,)), dma((2 * nz,)), dma((2 * nz,)),
-            dma((2 * nz,)), dma((6,)), dma((2,)),
+            dma((2 * nz,)), dma((11,)), dma((nz,)), dma((nz,)), dma((nz,)), dma((nz,)), dma((nz,)),
+            dma((3,)), dma((nz,)), dma((5,)), dma((3,)),
         ],
         compiler_params=pltpu.CompilerParams(
             collective_id=0, has_side_effects=True, vmem_limit_bytes=60 * 1024 * 1024
@@ -353,41 +600,12 @@
 
 
 def body(tokens, out_grad, probs, expert_ids, w_gate, w_up, w_down):
-    tok_rows = tokens.shape[1]
-    width = tokens.shape[2]
-    top_count = probs.shape[2]
-    experts = lax.axis_size("cp")
-    replicas = lax.axis_size("dp")
-    capacity = tok_rows * top_count * CAP_NUM // (CAP_DEN * experts)
-    columns = width // replicas
-    total_rows = experts * capacity
-    input_part, prob_part, gate_grad, up_grad, down_grad = expert_call(
+    passed, prob_grad, gate_grad, up_grad, down_grad = expert_call(
         tokens[0], out_grad[0], expert_ids[0].T, probs[0].T, w_gate[0, 0], w_up[0, 0], w_down[0, 0]
     )
-    reduced = lax.psum_scatter(input_part, "dp", scatter_dimension=1, tiled=True)
-    back = lax.all_to_all(
-        reduced.reshape(experts, capacity, columns), "cp", split_axis=0, concat_axis=0, tiled=True
-    )
-    back_probs = lax.all_to_all(
-        prob_part.reshape(experts, capacity), "cp", split_axis=0, concat_axis=0, tiled=True
-    )
-    back_probs = lax.psum(back_probs, "dp")
-    one_hot = expert_ids[0][:, :, None] == jnp.arange(experts)[None, None, :]
-    has_e = jnp.any(one_hot, axis=1).astype(jnp.int32)
-    slot_e = jnp.cumsum(has_e, axis=0) - has_e
-    pick_e = (slot_e[:, :, None] == jnp.arange(capacity)[None, None, :]) & (has_e[:, :, None] > 0)
-    input_sum = jnp.dot(
-        pick_e.reshape(tok_rows, total_rows).astype(jnp.bfloat16),
-        back.reshape(total_rows, columns),
-        preferred_element_type=jnp.float32,
-    )
-    prob_te = jnp.sum(jnp.where(pick_e, back_probs[None], 0.0), axis=2)
-    prob_grad = jnp.sum(jnp.where(one_hot, prob_te[:, None, :], 0.0), axis=2)
-    prob_grad = prob_grad / probs[0].astype(F32)
-    passed = lax.ppermute(input_sum.astype(jnp.bfloat16), "pp", [(1, 0)])
     return (
-        passed[None],
-        prob_grad[None],
+        passed.T[None],
+        prob_grad.T[None],
         gate_grad[None, None],
         up_grad[None, None],
         down_grad[None, None],

time: 225 us -> 148 us (0.66)
  the two profiles are of different devices: /device:TPU:8 before, /device:TPU:1 now
where the time goes in v3:
time: 148 us; the launch traced here: 147 us
  Pallas kernels  139 us (94%)
  local copies, waits for them, and re-layouts  7.92 us (5%)
    pallas_call x1, Pallas kernels, expert_call(): pl.pallas_call(functools.partial(expert_kernel, (tok_rows, width, experts...  139 us
    unnamed x9, local copies, waits for them, and re-layouts  7.92 us

profile of v3, /device:TPU:1, one launch (start us, length us, event | category | flops | bytes accessed | tf_op | source)
XLA Modules:
  0.0 147.3 jit_solution(16960805135530039572)
XLA Ops:
  0.6 138.7 %expert.1 = (bf16[448,128]{1,0:T(8,128)(2,1)}, f32[8,128]{1,0:T(8,128)}, bf16[160,3584]{1,0:T(8,128)(2,1)}, bf16[160,3584]{1,0:T(8,128)(2,1)}, bf16[160,3584]{1,0:T(8,128)(2,1)}) custom-call(bf16[128,3584]{1,0:T(8,128)(2,1)} %bitcast.26, bf16[128,3584]{1,0:T(8,128)(2,1)} %bitcast.27, s32[8,128]{1,0:T(8,128)} %bitcast.30, bf16[8,128]{1,0:T(8,128)(2,1)} %bitcast.31, ...), custom_call_target="tpu_custom_call" | custom-call | tf_op jit(solution)/shard_map/expert/pallas_call | solution.py:557
  139.4 1.6 %copy.17 = bf16[1,128,448]{1,2,0:T(8,128)(2,1)} copy(bf16[1,128,448]{1,2,0:T(8,128)(2,1)} %bitcast.28) | data formatting | bytes 229376
  140.9 1.3 copy.18
  142.2 0.0 copy-start.1
  142.2 2.4 %copy.19 = bf16[1,1,160,3584]{3,2,1,0:T(8,128)(2,1)} copy(bf16[1,1,160,3584]{3,2,1,0:T(8,128)(2,1)} %bitcast.22) | data formatting | bytes 2293760
  144.6 0.0 copy-done.1
  144.6 0.0 copy-start
  144.6 1.0 copy.20
  145.6 0.7 copy-done
  146.3 1.0 copy.21
Async XLA Ops:
  142.2 2.4 %copy-start.1 = (bf16[160,3584]{1,0:T(8,128)(2,1)S(1)}, bf16[160,3584]{1,0:T(8,128)(2,1)}, u32[]{:S(2)}) copy-start(bf16[160,3584]{1,0:T(8,128)(2,1)} %get-tuple-element.13) | copy-start | bytes 3440644
  144.6 1.7 %copy-start = (bf16[160,3584]{1,0:T(8,128)(2,1)S(1)}, bf16[160,3584]{1,0:T(8,128)(2,1)}, u32[]{:S(2)}) copy-start(bf16[160,3584]{1,0:T(8,128)(2,1)} %get-tuple-element.14) | copy-start | bytes 3440644

commit v4 on v3

--- a/solution.py
+++ b/solution.py
@@ -8,6 +8,7 @@
 
 CAP_NUM, CAP_DEN = 5, 4
 MESH = pl.DeviceIdType.MESH
+PROXIED = 3
 F32, BF16 = jnp.float32, jnp.bfloat16
 
 
@@ -15,8 +16,8 @@
     dims, tok, grd, ids, prb, w_gate, w_up, w_down,
     passed_out, prob_out, gg_out, ug_out, dg_out,
     blk, stg, xs, wg, wu, wd, hid, ggp, gup, grb, ipb, c1r, farr, comr, dirr, l3r,
-    ptab, prcv, pcol, pfin, fxs, fxr, fin, zero,
-    loc, zr, xr, cr, yt, yg, cf, snd, c1m, fam, com, dim, l3m, ppm, pcm, psn, one,
+    ptab, prcv, pcol, pfin, fxs, fxr, tab,
+    loc, zr, xr, cr, yt, yg, cf, snd, c1m, fam, com, dim, l3m, pxm, ppm, pcm, psn, one,
 ):
     tok_rows, width, experts, cap, nz, ny = dims
     quarter = width // 4
@@ -46,14 +47,22 @@
     def owner(zz):
         return {"cp": zz * 2 + core, "dp": owner_dp}
 
+    def other_owner(zz):
+        return {"pp": 1 - pp, "cp": zz * 2 + core, "dp": owner_dp}
+
+    proxy = {"pp": 1 - pp, "cp": cp_x}
+
     barrier = pltpu.get_barrier_semaphore()
     for where in (
         {"cp": cp_x}, {"cp": z_up}, {"cp": z_dn}, {"dp": dp_c}, {"dp": y_up}, {"dp": y_dn},
-        {"pp": 1 - pp},
+        {"pp": 1 - pp}, proxy,
     ):
         pl.semaphore_signal(barrier, inc=1, device_id=where, device_id_type=MESH)
-    for dz in range(1, nz):
-        pl.semaphore_signal(barrier, inc=1, device_id=owner((z + dz) % nz), device_id_type=MESH)
+    for dz in range(nz):
+        zz = (z + dz) % nz
+        pl.semaphore_signal(barrier, inc=1, device_id=other_owner(zz), device_id_type=MESH)
+        if dz:
+            pl.semaphore_signal(barrier, inc=1, device_id=owner(zz), device_id_type=MESH)
 
     @pl.when(jnp.logical_not(same))
     def _():
@@ -100,8 +109,7 @@
     for c in loads:
         c.wait()
     ptab[...] = jnp.zeros_like(ptab)
-    zero[...] = jnp.zeros_like(zero)
-    pl.semaphore_wait(barrier, 7 + nz - 1 + jnp.where(same, 0, 1))
+    pl.semaphore_wait(barrier, 8 + 2 * nz - 1 + jnp.where(same, 0, 1))
 
     def remote(src, dst, s, r, where):
         return pltpu.make_async_remote_copy(
@@ -110,6 +118,13 @@
 
     first, second = pl.ds(0, half_pay), pl.ds(half_pay, tok_rows)
     s_z, s_x, s_c, s_t, s_g, s_f = (snd.at[j] for j in range(6))
+    slots_copy = remote(
+        blk.at[z, pl.ds(tok_rows, route), pl.ds(0, tok_rows)], tab, snd.at[9], one.at[1], {"pp": 0}
+    )
+
+    @pl.when(returns)
+    def _():
+        slots_copy.start()
 
     def z_at(i):
         away = (i + 1) // 2
@@ -241,16 +256,30 @@
         direct = remote(ipb.at[i, rows, ccols(bwd_y)], dirr.at[i], s_y, dim.at[i], bwd_to)
         return far, comb, direct, fwd_y, rows
 
-    def owner_copy(i):
+    def owner_copy(i, where):
         rows = pl.ds(pl.multiple_of(core * cap, 16), cap)
-        return remote(
-            ipb.at[i, rows, ccols(y)], l3r.at[z], snd.at[8], l3m.at[z], owner(z_at(i))
-        )
+        return remote(ipb.at[i, rows, ccols(y)], l3r.at[z], snd.at[8], l3m.at[z], where)
+
+    def proxy_copy(i):
+        return remote(mine_of(i), mine_of(i), snd.at[10], pxm.at[i], proxy)
 
     def ret_a(i):
         core_sum(i).wait_recv()
         rows = pl.ds(pl.multiple_of(core * cap, 16), cap)
         ipb[i, rows, :] = (ipb[i, rows, :].astype(F32) + c1r[i].astype(F32)).astype(BF16)
+
+        @pl.when(i < PROXIED)
+        def _():
+            proxy_copy(i).start()
+
+        @pl.when(i >= PROXIED)
+        def _():
+            far, _, direct, _, _ = y_steps(i)
+            far.start()
+            direct.start()
+
+    def proxy_a(i):
+        proxy_copy(i).wait_recv()
         far, _, direct, _, _ = y_steps(i)
         far.start()
         direct.start()
@@ -267,7 +296,7 @@
         comb.wait_recv()
         direct.wait_recv()
         total = ipb[i, rows, ccols(y)].astype(F32) + comr[i].astype(F32) + dirr[i].astype(F32)
-        here = same & (i == 0)
+        here = same & (i == 0) & jnp.logical_not(returns)
 
         @pl.when(here)
         def _():
@@ -276,7 +305,14 @@
         @pl.when(jnp.logical_not(here))
         def _():
             ipb[i, rows, ccols(y)] = total.astype(BF16)
-            owner_copy(i).start()
+
+            @pl.when(returns)
+            def _():
+                owner_copy(i, {"pp": 0, **owner(z_at(i))}).start()
+
+            @pl.when(jnp.logical_not(returns))
+            def _():
+                owner_copy(i, owner(z_at(i))).start()
 
     def compute(i):
         zz = z_at(i)
@@ -343,9 +379,8 @@
         def _():
             pcol[z] = ptab[3, z * 2 + core]
 
-    def own_hits(zz):
-        table = blk[z, tok_rows:half_pay, 0:tok_rows].astype(F32)
-        row = jnp.sum(jnp.where(e_iota == zz * 2 + core, table, 0.0), axis=0, keepdims=True)
+    def own_hits(table, expert):
+        row = jnp.sum(jnp.where(e_iota == expert, table, 0.0), axis=0, keepdims=True)
         c_iota = lax.broadcasted_iota(jnp.int32, (cap, tok_rows), 0).astype(F32)
         return jnp.where(c_iota == row, 1.0, 0.0).astype(BF16)
 
@@ -363,11 +398,12 @@
     def prob_pick():
         each_source(pcol, pcm, psn.at[3])
         acc = jnp.zeros(id_val.shape, F32)
+        table = blk[z, tok_rows:half_pay, 0:tok_rows].astype(F32)
         for zz in range(nz):
             val = pcol[zz][:, 0:cap]
             high = val.astype(BF16)
             low = (val - high.astype(F32)).astype(BF16)
-            hits = own_hits(zz)
+            hits = own_hits(table, zz * 2 + core)
             got = jnp.dot(high, hits, preferred_element_type=F32)
             got += jnp.dot(low, hits, preferred_element_type=F32)
             acc = jnp.where(ids[...] == zz * 2 + core, got, acc)
@@ -414,11 +450,17 @@
             for c in weights:
                 c.wait()
 
-        for lag, stage in ((9, ret_c), (7, ret_b), (5, ret_a)):
-
-            @pl.when(returns & (i >= lag) & (i < nz + lag))
+        for lag, low, stage in ((9, PROXIED, ret_c), (7, PROXIED, ret_b), (5, 0, ret_a)):
+
+            @pl.when(returns & (i >= lag + low) & (i < nz + lag))
             def _(lag=lag, stage=stage):
                 stage(i - lag)
+
+        for lag, stage in ((14, ret_c), (12, ret_b), (10, proxy_a)):
+
+            @pl.when(jnp.logical_not(returns) & (i >= lag) & (i < 2 * PROXIED + lag) & (i % 2 == 0))
+            def _(lag=lag, stage=stage):
+                stage((i - lag) // 2)
 
         @pl.when((i >= 4) & (i < nz + 4))
         def _():
@@ -459,17 +501,31 @@
     ]
     for c in outs:
         c.start()
-    hand_over = remote(fin, passed_out, snd.at[9], one.at[1], {"pp": 0})
-    swap = remote(fxs, fxr, snd.at[10], one.at[2], {"dp": dp_c})
-    blank = pltpu.make_async_copy(zero, passed_out, loc.at[3])
+    swap = remote(fxs, fxr, snd.at[11], one.at[2], {"dp": dp_c})
 
     @pl.when(returns)
     def _():
-        blank.start()
-        each_source(l3r, l3m, snd.at[8])
-        hits = jnp.concatenate([own_hits(zz) for zz in range(nz)], axis=0)
-        rows = jnp.concatenate([l3r[zz] for zz in range(nz)], axis=0)
-        tot = lax.dot_general(hits, rows, by_row, preferred_element_type=F32).T
+        passed_out[...] = jnp.zeros_like(passed_out)
+
+    @pl.when(jnp.logical_not(returns))
+    def _():
+        slots_copy.wait_recv()
+        table = tab[...].astype(F32)
+        hits, rows = [], []
+        for i in range(nz):
+            away = (i + 1) // 2
+            src = (z + nz + (away if i % 2 == 1 else -away)) % nz
+            landed = remote(l3r.at[src], l3r.at[src], snd.at[8], l3m.at[src], owner(z))
+            if i == 0:
+                pl.when(jnp.logical_not(same))(landed.wait_recv)
+            else:
+                landed.wait_recv()
+            hits.append(own_hits(table, src * 2 + (1 - core if i < PROXIED else core)))
+            rows.append(l3r[src])
+        tot = lax.dot_general(
+            jnp.concatenate(hits, axis=0), jnp.concatenate(rows, axis=0), by_row,
+            preferred_element_type=F32,
+        ).T
 
         @pl.when(core == 0)
         def _():
@@ -482,8 +538,7 @@
         swap.start()
         kept = jnp.where(core == 0, tot[:half_w], tot[half_w:])
         swap.wait_recv()
-        fin[...] = (kept + fxr[...]).astype(BF16)
-        hand_over.start()
+        passed_out[...] = (kept + fxr[...]).astype(BF16)
 
     last_copy.wait_recv()
     prob_out[...] = (pfin[0] + pfin[1]) / prb[...].astype(F32)
@@ -512,29 +567,33 @@
     def _():
         remote(pcol, pcol, psn.at[3], one.at[0], owner(z)).wait_send()
 
+    def sent_pieces(pieces, sem):
+        ref = dirr.at[pl.ds(0, pieces)]
+        remote(ref, ref, sem, one.at[0], {"dp": y_up}).wait_send()
+
     @pl.when(returns)
     def _():
         remote(c1r, c1r, snd.at[6], one.at[0], {"dp": dp_c}).wait_send()
-        total = farr.shape[0] * 3 * chunk // (2 * width)
-        sent = ipb.at[pl.ds(0, total)]
-        remote(sent, sent, snd.at[7], one.at[0], {"dp": y_up}).wait_send()
+        ref = c1r.at[pl.ds(0, PROXIED)]
+        remote(ref, ref, snd.at[10], one.at[0], proxy).wait_send()
+        many = ipb.at[pl.ds(0, nz - PROXIED), pl.ds(0, cap), pl.ds(0, 3 * chunk)]
+        remote(many, many, snd.at[7], one.at[0], {"dp": y_up}).wait_send()
+        sent_pieces(nz - PROXIED, snd.at[8])
+        slots_copy.wait_send()
+
+    @pl.when(jnp.logical_not(returns))
+    def _():
+        many = ipb.at[pl.ds(0, PROXIED), pl.ds(0, cap), pl.ds(0, 3 * chunk)]
+        remote(many, many, snd.at[7], one.at[0], {"dp": y_up}).wait_send()
         swap.wait_send()
-        hand_over.wait_send()
-        blank.wait()
-
-    seven_l = l3r.at[pl.ds(0, nz - 1)]
-
-    @pl.when(returns & same)
-    def _():
-        remote(seven_l, seven_l, snd.at[8], one.at[0], owner(z)).wait_send()
-
-    @pl.when(returns & jnp.logical_not(same))
-    def _():
-        remote(l3r, l3r, snd.at[8], one.at[0], owner(z)).wait_send()
-
-    @pl.when(jnp.logical_not(returns))
-    def _():
-        hand_over.wait_recv()
+
+    @pl.when(jnp.logical_not(returns) & same)
+    def _():
+        sent_pieces(PROXIED - 1, snd.at[8])
+
+    @pl.when(jnp.logical_not(returns) & jnp.logical_not(same))
+    def _():
+        sent_pieces(PROXIED, snd.at[8])
 
     for c in outs:
         c.wait()
@@ -562,7 +621,7 @@
             wshape, wshape, wshape,
         ),
         in_specs=[anyspace, anyspace, vmem, vmem, anyspace, anyspace, anyspace],
-        out_specs=(anyspace, vmem, anyspace, anyspace, anyspace),
+        out_specs=(vmem, vmem, anyspace, anyspace, anyspace),
         scratch_shapes=[
             pltpu.VMEM((nz, pay, quarter), BF16),
             pltpu.VMEM((nz, 2, cap, quarter), BF16),
@@ -586,11 +645,10 @@
             pltpu.VMEM((2, top, tok_rows), F32),
             pltpu.VMEM((width // (2 * ny), tok_rows), F32),
             pltpu.VMEM((width // (2 * ny), tok_rows), F32),
-            pltpu.VMEM((width // (2 * ny), tok_rows), BF16),
-            pltpu.VMEM((width // (2 * ny), tok_rows), BF16),
+            pltpu.VMEM((16, tok_rows), BF16),
             dma((5,)), dma((9,)), dma((nz,)), dma((2 * nz,)), dma((2 * nz,)), dma((2 * nz,)),
-            dma((2 * nz,)), dma((11,)), dma((nz,)), dma((nz,)), dma((nz,)), dma((nz,)), dma((nz,)),
-            dma((3,)), dma((nz,)), dma((5,)), dma((3,)),
+            dma((2 * nz,)), dma((12,)), dma((nz,)), dma((nz,)), dma((nz,)), dma((nz,)), dma((nz,)),
+            dma((PROXIED,)), dma((3,)), dma((nz,)), dma((5,)), dma((3,)),
         ],
         compiler_params=pltpu.CompilerParams(
             collective_id=0, has_side_effects=True, vmem_limit_bytes=60 * 1024 * 1024

time: 148 us -> 130 us (0.88)
  Pallas kernels: 139 us -> 121 us
    pallas_call x1, Pallas kernels: 139 us -> 121 us  [expert_call(): pl.pallas_call(functools.partial(expert_kernel, (tok_rows, width, experts...]
where the time goes in v4:
time: 130 us
  Pallas kernels  121 us (93%)
  local copies, waits for them, and re-layouts  7.92 us (6%)
    pallas_call x1, Pallas kernels, expert_call(): pl.pallas_call(functools.partial(expert_kernel, (tok_rows, width, experts...  121 us
    unnamed x9, local copies, waits for them, and re-layouts  7.92 us

profile of v4, /device:TPU:1, one launch (start us, length us, event | category | flops | bytes accessed | tf_op | source)
XLA Modules:
  0.0 129.8 jit_solution(17588206226514918047)
XLA Ops:
  0.6 121.3 %expert.1 = (bf16[448,128]{1,0:T(8,128)(2,1)}, f32[8,128]{1,0:T(8,128)}, bf16[160,3584]{1,0:T(8,128)(2,1)}, bf16[160,3584]{1,0:T(8,128)(2,1)}, bf16[160,3584]{1,0:T(8,128)(2,1)}) custom-call(bf16[128,3584]{1,0:T(8,128)(2,1)} %bitcast.26, bf16[128,3584]{1,0:T(8,128)(2,1)} %bitcast.27, s32[8,128]{1,0:T(8,128)} %bitcast.30, bf16[8,128]{1,0:T(8,128)(2,1)} %bitcast.31, ...), custom_call_target="tpu_custom_call" | custom-call | tf_op jit(solution)/shard_map/expert/pallas_call | solution.py:616
  121.9 1.6 %copy.17 = bf16[1,128,448]{1,2,0:T(8,128)(2,1)} copy(bf16[1,128,448]{1,2,0:T(8,128)(2,1)} %bitcast.28) | data formatting | bytes 229376
  123.5 1.3 copy.18
  124.7 0.0 copy-start.1
  124.7 2.4 %copy.19 = bf16[1,1,160,3584]{3,2,1,0:T(8,128)(2,1)} copy(bf16[1,1,160,3584]{3,2,1,0:T(8,128)(2,1)} %bitcast.22) | data formatting | bytes 2293760
  127.1 0.0 copy-done.1
  127.2 0.0 copy-start
  127.2 1.0 copy.20
  128.2 0.7 copy-done
  128.8 1.0 copy.21
Async XLA Ops:
  124.7 2.4 %copy-start.1 = (bf16[160,3584]{1,0:T(8,128)(2,1)S(1)}, bf16[160,3584]{1,0:T(8,128)(2,1)}, u32[]{:S(2)}) copy-start(bf16[160,3584]{1,0:T(8,128)(2,1)} %get-tuple-element.13) | copy-start | bytes 3440644
  127.2 1.7 %copy-start = (bf16[160,3584]{1,0:T(8,128)(2,1)S(1)}, bf16[160,3584]{1,0:T(8,128)(2,1)}, u32[]{:S(2)}) copy-start(bf16[160,3584]{1,0:T(8,128)(2,1)} %get-tuple-element.14) | copy-start | bytes 3440644

commit v5 on v4

--- a/solution.py
+++ b/solution.py
@@ -15,9 +15,9 @@
 def expert_kernel(
     dims, tok, grd, ids, prb, w_gate, w_up, w_down,
     passed_out, prob_out, gg_out, ug_out, dg_out,
-    blk, stg, xs, wg, wu, wd, hid, ggp, gup, grb, ipb, c1r, farr, comr, dirr, l3r,
-    ptab, prcv, pcol, pfin, fxs, fxr, tab,
-    loc, zr, xr, cr, yt, yg, cf, snd, c1m, fam, com, dim, l3m, pxm, ppm, pcm, psn, one,
+    blk, stg, xs, wg, wu, wd, hid, ggp, gup, ipb, c1r, farr, comr, dirr, l3r,
+    ptab, pcol, pall, fxs, fxr, tab,
+    loc, zr, xr, cr, yt, yg, cf, snd, c1m, fam, com, dim, l3m, pxm, pcm, pam, psn, one,
 ):
     tok_rows, width, experts, cap, nz, ny = dims
     quarter = width // 4
@@ -53,20 +53,23 @@
     proxy = {"pp": 1 - pp, "cp": cp_x}
 
     barrier = pltpu.get_barrier_semaphore()
-    for where in (
-        {"cp": cp_x}, {"cp": z_up}, {"cp": z_dn}, {"dp": dp_c}, {"dp": y_up}, {"dp": y_dn},
-        {"pp": 1 - pp}, proxy,
-    ):
+
+    def greet(where):
         pl.semaphore_signal(barrier, inc=1, device_id=where, device_id_type=MESH)
-    for dz in range(nz):
-        zz = (z + dz) % nz
-        pl.semaphore_signal(barrier, inc=1, device_id=other_owner(zz), device_id_type=MESH)
-        if dz:
-            pl.semaphore_signal(barrier, inc=1, device_id=owner(zz), device_id_type=MESH)
+
+    for d in range(1, ncp):
+        greet({"cp": (cp + d) % ncp})
+    for d in range(1, ndp):
+        greet({"dp": (dp + d) % ndp})
+    greet({"pp": 1 - pp})
+    greet(proxy)
+    for zz in range(nz):
+        greet(other_owner(zz))
 
     @pl.when(jnp.logical_not(same))
     def _():
-        pl.semaphore_signal(barrier, inc=1, device_id=owner(z), device_id_type=MESH)
+        for zz in range(nz):
+            greet(owner(zz))
 
     loads = [
         pltpu.make_async_copy(
@@ -109,7 +112,7 @@
     for c in loads:
         c.wait()
     ptab[...] = jnp.zeros_like(ptab)
-    pl.semaphore_wait(barrier, 8 + 2 * nz - 1 + jnp.where(same, 0, 1))
+    pl.semaphore_wait(barrier, ncp + ndp + nz + jnp.where(same, 0, nz))
 
     def remote(src, dst, s, r, where):
         return pltpu.make_async_remote_copy(
@@ -313,6 +316,20 @@
             @pl.when(jnp.logical_not(returns))
             def _():
                 owner_copy(i, owner(z_at(i))).start()
+
+    def prob_send(i, k):
+        zz = z_at(i)
+        here = (i == 0) & (xl == k)
+
+        @pl.when(here)
+        def _():
+            pcol[cp] = ptab[cp]
+
+        @pl.when(jnp.logical_not(here))
+        def _():
+            remote(
+                ptab.at[zz * 2 + k], pcol.at[cp], psn.at[0], pcm.at[cp], {"cp": zz * 2 + k}
+            ).start()
 
     def compute(i):
         zz = z_at(i)
@@ -338,7 +355,8 @@
             part = slice(k * cap, (k + 1) * cap)
             sums = lax.dot_general(ones, high[part], by_feature, preferred_element_type=F32)
             sums += lax.dot_general(ones, low[part], by_feature, preferred_element_type=F32)
-            ptab[0, zz * 2 + k, :, 0:cap] = sums
+            ptab[zz * 2 + k, :, 0:cap] = sums
+            prob_send(i, k)
         g_gate = (g_hid * up_pre * sigma * (1.0 + gate_pre * (1.0 - sigma))).astype(BF16)
         g_up = (g_hid * silu).astype(BF16)
         ggp[rows, :] = g_gate
@@ -353,62 +371,45 @@
                 ipb[i, :, lo : lo + step] = part.astype(BF16)
             core_sum(i).start()
 
-    def pair_copy(r):
-        to = (dp_c, (y + 1 - 2 * (y % 2)) * 2 + core, (ny - 1 - y) * 2 + core)[r]
-        return remote(ptab.at[r], prcv.at[r], psn.at[r], ppm.at[r], {"dp": to})
-
-    def pair_sum(r):
-        pair_copy(r).wait_recv()
-        ptab[r + 1] = ptab[r] + prcv[r]
-
-    def prob_copy(dz):
-        zz = (z + dz) % nz
-        return remote(
-            ptab.at[3, zz * 2 + core], pcol.at[z], psn.at[3], pcm.at[z], owner(zz)
-        )
-
-    def prob_spread():
-        for dz in range(1, nz):
-            prob_copy(dz).start()
-
-        @pl.when(jnp.logical_not(same))
-        def _():
-            prob_copy(0).start()
-
-        @pl.when(same)
-        def _():
-            pcol[z] = ptab[3, z * 2 + core]
-
     def own_hits(table, expert):
         row = jnp.sum(jnp.where(e_iota == expert, table, 0.0), axis=0, keepdims=True)
         c_iota = lax.broadcasted_iota(jnp.int32, (cap, tok_rows), 0).astype(F32)
         return jnp.where(c_iota == row, 1.0, 0.0).astype(BF16)
 
-    def each_source(ref, sems, sem):
-        for dz in range(1, nz):
-            src = (z + dz) % nz
-            remote(ref.at[src], ref.at[src], sem, sems.at[src], owner(z)).wait_recv()
-
-        @pl.when(jnp.logical_not(same))
-        def _():
-            remote(ref.at[z], ref.at[z], sem, sems.at[z], owner(z)).wait_recv()
-
-    last_copy = remote(pfin.at[0], pfin.at[1], psn.at[4], one.at[0], {"dp": dp_c})
+    def dp_copy(d):
+        return remote(
+            pall.at[dp], pall.at[dp], psn.at[1], pam.at[dp], {"dp": (dp + d) % ndp}
+        )
 
     def prob_pick():
-        each_source(pcol, pcm, psn.at[3])
+        for d in range(1, ncp):
+            src = (cp + d) % ncp
+            remote(
+                pcol.at[src], pcol.at[src], psn.at[0], pcm.at[src], {"cp": src}
+            ).wait_recv()
         acc = jnp.zeros(id_val.shape, F32)
         table = blk[z, tok_rows:half_pay, 0:tok_rows].astype(F32)
-        for zz in range(nz):
-            val = pcol[zz][:, 0:cap]
+        for expert in range(experts):
+            val = pcol[expert][:, 0:cap]
             high = val.astype(BF16)
             low = (val - high.astype(F32)).astype(BF16)
-            hits = own_hits(table, zz * 2 + core)
+            hits = own_hits(table, expert)
             got = jnp.dot(high, hits, preferred_element_type=F32)
             got += jnp.dot(low, hits, preferred_element_type=F32)
-            acc = jnp.where(ids[...] == zz * 2 + core, got, acc)
-        pfin[0] = acc
-        last_copy.start()
+            acc = jnp.where(ids[...] == expert, got, acc)
+        pall[dp] = acc
+        for d in range(1, ndp):
+            dp_copy(d).start()
+
+    def prob_finish():
+        total = pall[dp]
+        for d in range(1, ndp):
+            src = (dp + d) % ndp
+            remote(
+                pall.at[src], pall.at[src], psn.at[1], pam.at[src], {"dp": src}
+            ).wait_recv()
+            total += pall[src]
+        prob_out[...] = total / prb[...].astype(F32)
 
     grad_step = 512
     n_grad = width // grad_step
@@ -416,13 +417,13 @@
     def grads(t):
         cols = pl.ds(pl.multiple_of(t * grad_step, 128), grad_step)
         x_cols = xs[0, :, cols]
-        grb[0, :, cols] = lax.dot_general(
+        gg_out[:, cols] = lax.dot_general(
             ggp[...], x_cols, by_row, preferred_element_type=F32
         ).astype(BF16)
-        grb[1, :, cols] = lax.dot_general(
+        ug_out[:, cols] = lax.dot_general(
             gup[...], x_cols, by_row, preferred_element_type=F32
         ).astype(BF16)
-        grb[2, :, cols] = lax.dot_general(
+        dg_out[:, cols] = lax.dot_general(
             hid[...], xs[1, :, cols], by_row, preferred_element_type=F32
         ).astype(BF16)
 
@@ -468,23 +469,7 @@
 
         first_free = nz + 4
 
-        @pl.when(i == first_free)
-        def _():
-            pair_copy(0).start()
-
-        for r in (0, 1):
-
-            @pl.when(i == first_free + 1 + r)
-            def _(r=r):
-                pair_sum(r)
-                pair_copy(r + 1).start()
-
-        @pl.when(i == first_free + 3)
-        def _():
-            pair_sum(2)
-            prob_spread()
-
-        @pl.when(i == first_free + 5)
+        @pl.when(i == first_free + 4)
         def _():
             prob_pick()
 
@@ -496,11 +481,6 @@
 
     lax.fori_loop(0, nz + 4 + n_grad, step_fn, 0)
 
-    outs = [
-        pltpu.make_async_copy(grb.at[j], o, loc.at[j]) for j, o in enumerate((gg_out, ug_out, dg_out))
-    ]
-    for c in outs:
-        c.start()
     swap = remote(fxs, fxr, snd.at[11], one.at[2], {"dp": dp_c})
 
     @pl.when(returns)
@@ -540,8 +520,7 @@
         swap.wait_recv()
         passed_out[...] = (kept + fxr[...]).astype(BF16)
 
-    last_copy.wait_recv()
-    prob_out[...] = (pfin[0] + pfin[1]) / prb[...].astype(F32)
+    prob_finish()
     cols, ocols = pl.ds(mine_q, quarter), pl.ds(other_q, quarter)
     seven = blk.at[pl.ds(0, nz - 1)]
     remote(seven, seven, s_z, zr.at[0], {"cp": z_up}).wait_send()
@@ -554,18 +533,10 @@
     remote(a, a, s_g, zr.at[0], {"dp": y_dn}).wait_send()
     a = xs.at[:, :, ocols]
     remote(a, a, s_f, zr.at[0], {"dp": dp_c}).wait_send()
-    for r in (0, 1, 2):
-        pair_copy(r).wait_send()
-    last_copy.wait_send()
-    seven_p = pcol.at[pl.ds(0, nz - 1)]
-
-    @pl.when(same)
-    def _():
-        remote(seven_p, seven_p, psn.at[3], one.at[0], owner(z)).wait_send()
-
-    @pl.when(jnp.logical_not(same))
-    def _():
-        remote(pcol, pcol, psn.at[3], one.at[0], owner(z)).wait_send()
+    most = pcol.at[pl.ds(0, experts - 1)]
+    remote(most, most, psn.at[0], one.at[0], {"cp": z_up}).wait_send()
+    most = pall.at[pl.ds(0, ndp - 1)]
+    remote(most, most, psn.at[1], one.at[0], {"dp": y_up}).wait_send()
 
     def sent_pieces(pieces, sem):
         ref = dirr.at[pl.ds(0, pieces)]
@@ -594,9 +565,6 @@
     @pl.when(jnp.logical_not(returns) & jnp.logical_not(same))
     def _():
         sent_pieces(PROXIED, snd.at[8])
-
-    for c in outs:
-        c.wait()
 
 
 def expert_call(tokens, out_grad, ids_t, probs_t, w_gate, w_up, w_down):
@@ -611,17 +579,17 @@
     pay = 2 * tok_rows + 16
     anyspace = pl.BlockSpec(memory_space=pl.ANY)
     vmem = pl.BlockSpec(memory_space=pltpu.VMEM)
-    wshape = jax.ShapeDtypeStruct((ff, width), BF16)
+    wshape = pltpu.VMEM((ff, width), BF16)
     dma = pltpu.SemaphoreType.DMA
     return pl.pallas_call(
         functools.partial(expert_kernel, (tok_rows, width, experts, cap, nz, ny)),
         out_shape=(
-            jax.ShapeDtypeStruct((width // (2 * ny), tok_rows), BF16),
-            jax.ShapeDtypeStruct((top, tok_rows), F32),
+            pltpu.VMEM((width // (2 * ny), tok_rows), BF16),
+            pltpu.VMEM((top, tok_rows), F32),
             wshape, wshape, wshape,
         ),
         in_specs=[anyspace, anyspace, vmem, vmem, anyspace, anyspace, anyspace],
-        out_specs=(vmem, vmem, anyspace, anyspace, anyspace),
+        out_specs=(vmem,) * 5,
         scratch_shapes=[
             pltpu.VMEM((nz, pay, quarter), BF16),
             pltpu.VMEM((nz, 2, cap, quarter), BF16),
@@ -632,23 +600,21 @@
             pltpu.VMEM((rows, ff), BF16),
             pltpu.VMEM((rows, ff), BF16),
             pltpu.VMEM((rows, ff), BF16),
-            pltpu.VMEM((3, ff, width), BF16),
             pltpu.VMEM((nz, 2 * cap, width), BF16),
             pltpu.VMEM((nz, cap, width), BF16),
             pltpu.VMEM((nz, cap, width // ny), BF16),
             pltpu.VMEM((nz, cap, width // ny), BF16),
             pltpu.VMEM((nz, cap, width // ny), BF16),
             pltpu.VMEM((nz, cap, width // ny), BF16),
-            pltpu.VMEM((4, experts, 8, 128), F32),
-            pltpu.VMEM((3, experts, 8, 128), F32),
-            pltpu.VMEM((nz, 8, 128), F32),
-            pltpu.VMEM((2, top, tok_rows), F32),
+            pltpu.VMEM((experts, 8, 128), F32),
+            pltpu.VMEM((experts, 8, 128), F32),
+            pltpu.VMEM((ny * 2, top, tok_rows), F32),
             pltpu.VMEM((width // (2 * ny), tok_rows), F32),
             pltpu.VMEM((width // (2 * ny), tok_rows), F32),
             pltpu.VMEM((16, tok_rows), BF16),
             dma((5,)), dma((9,)), dma((nz,)), dma((2 * nz,)), dma((2 * nz,)), dma((2 * nz,)),
             dma((2 * nz,)), dma((12,)), dma((nz,)), dma((nz,)), dma((nz,)), dma((nz,)), dma((nz,)),
-            dma((PROXIED,)), dma((3,)), dma((nz,)), dma((5,)), dma((3,)),
+            dma((PROXIED,)), dma((experts,)), dma((2 * ny,)), dma((2,)), dma((3,)),
         ],
         compiler_params=pltpu.CompilerParams(
             collective_id=0, has_side_effects=True, vmem_limit_bytes=60 * 1024 * 1024

time: 130 us -> 126 us (0.969)
  local copies, waits for them, and re-layouts: 7.92 us -> 4.25 us
    unnamed x9 -> x5, local copies, waits for them, and re-layouts: 7.92 us -> 4.25 us
where the time goes in v5:
time: 126 us
  Pallas kernels  121 us (96%)
  local copies, waits for them, and re-layouts  4.25 us (3%)
    pallas_call x1, Pallas kernels, expert_call(): pl.pallas_call(functools.partial(expert_kernel, (tok_rows, width, experts...  121 us
    unnamed x5, local copies, waits for them, and re-layouts  4.25 us

profile of v5, /device:TPU:1, one launch (start us, length us, event | category | flops | bytes accessed | tf_op | source)
XLA Modules:
  0.0 125.9 jit_solution(6159152397227268157)
XLA Ops:
  0.6 121.1 %expert.1 = (bf16[448,128]{1,0:T(8,128)(2,1)S(1)}, f32[8,128]{1,0:T(8,128)S(1)}, bf16[160,3584]{1,0:T(8,128)(2,1)S(1)}, bf16[160,3584]{1,0:T(8,128)(2,1)S(1)}, bf16[160,3584]{1,0:T(8,128)(2,1)S(1)}) custom-call(bf16[128,3584]{1,0:T(8,128)(2,1)} %bitcast.28, bf16[128,3584]{1,0:T(8,128)(2,1)} %bitcast.29, s32[8,128]{1,0:T(8,128)} %bitcast.30, ...), custom_call_target="tpu_custom_call" | custom-call | tf_op jit(solution)/shard_map/expert/pallas_call | solution.py:584
  121.7 0.6 copy.17
  122.3 0.6 copy.18
  122.9 1.0 copy.19
  123.9 1.0 copy.20
  124.9 1.0 copy.21

commit v6 on v5

--- a/solution.py
+++ b/solution.py
@@ -473,13 +473,15 @@
         def _():
             prob_pick()
 
-        @pl.when(i >= first_free)
-        def _():
-            grads(i - first_free)
+        first_grad = first_free + jnp.where(returns, 5, 0)
+
+        @pl.when((i >= first_grad) & (i < first_grad + n_grad))
+        def _():
+            grads(i - first_grad)
 
         return carry
 
-    lax.fori_loop(0, nz + 4 + n_grad, step_fn, 0)
+    lax.fori_loop(0, nz + 4 + 5 + n_grad, step_fn, 0)
 
     swap = remote(fxs, fxr, snd.at[11], one.at[2], {"dp": dp_c})
 
@@ -491,7 +493,7 @@
     def _():
         slots_copy.wait_recv()
         table = tab[...].astype(F32)
-        hits, rows = [], []
+        tot = jnp.zeros((chunk, tok_rows), F32)
         for i in range(nz):
             away = (i + 1) // 2
             src = (z + nz + (away if i % 2 == 1 else -away)) % nz
@@ -500,12 +502,8 @@
                 pl.when(jnp.logical_not(same))(landed.wait_recv)
             else:
                 landed.wait_recv()
-            hits.append(own_hits(table, src * 2 + (1 - core if i < PROXIED else core)))
-            rows.append(l3r[src])
-        tot = lax.dot_general(
-            jnp.concatenate(hits, axis=0), jnp.concatenate(rows, axis=0), by_row,
-            preferred_element_type=F32,
-        ).T
+            hits = own_hits(table, src * 2 + (1 - core if i < PROXIED else core))
+            tot += lax.dot_general(l3r[src], hits, by_row, preferred_element_type=F32)
 
         @pl.when(core == 0)
         def _():

time: 126 us -> 126 us (level)
  no operation moved by 1% of the time
where the time goes in v6:
time: 126 us
  Pallas kernels  121 us (96%)
  local copies, waits for them, and re-layouts  4.25 us (3%)
    pallas_call x1, Pallas kernels, expert_call(): pl.pallas_call(functools.partial(expert_kernel, (tok_rows, width, experts...  121 us
    unnamed x5, local copies, waits for them, and re-layouts  4.25 us

profile of v6, /device:TPU:1, one launch (start us, length us, event | category | flops | bytes accessed | tf_op | source)
XLA Modules:
  0.0 125.7 jit_solution(6104237601887126716)
XLA Ops:
  0.6 120.8 %expert.1 = (bf16[448,128]{1,0:T(8,128)(2,1)S(1)}, f32[8,128]{1,0:T(8,128)S(1)}, bf16[160,3584]{1,0:T(8,128)(2,1)S(1)}, bf16[160,3584]{1,0:T(8,128)(2,1)S(1)}, bf16[160,3584]{1,0:T(8,128)(2,1)S(1)}) custom-call(bf16[128,3584]{1,0:T(8,128)(2,1)} %bitcast.28, bf16[128,3584]{1,0:T(8,128)(2,1)} %bitcast.29, s32[8,128]{1,0:T(8,128)} %bitcast.30, ...), custom_call_target="tpu_custom_call" | custom-call | tf_op jit(solution)/shard_map/expert/pallas_call | solution.py:582
  121.4 0.6 copy.17
  122.1 0.6 copy.18
  122.7 1.0 copy.19
  123.7 1.0 copy.20
  124.7 1.0 copy.21

commit v7 on v6

--- a/solution.py
+++ b/solution.py
@@ -428,6 +428,10 @@
         ).astype(BF16)
 
     def step_fn(i, carry):
+        @pl.when(returns & (i >= 5) & (i < nz + 5))
+        def _():
+            ret_a(i - 5)
+
         @pl.when(i < nz)
         def _():
             stage_block(i)
@@ -451,7 +455,7 @@
             for c in weights:
                 c.wait()
 
-        for lag, low, stage in ((9, PROXIED, ret_c), (7, PROXIED, ret_b), (5, 0, ret_a)):
+        for lag, low, stage in ((9, PROXIED, ret_c), (7, PROXIED, ret_b)):
 
             @pl.when(returns & (i >= lag + low) & (i < nz + lag))
             def _(lag=lag, stage=stage):

time: 126 us -> 128 us (1.016)
  Pallas kernels: 121 us -> 123 us
    pallas_call x1, Pallas kernels: 121 us -> 123 us  [expert_call(): pl.pallas_call(functools.partial(expert_kernel, (tok_rows, width, experts...]
where the time goes in v7:
time: 128 us
  Pallas kernels  123 us (96%)
  local copies, waits for them, and re-layouts  4.25 us (3%)
    pallas_call x1, Pallas kernels, expert_call(): pl.pallas_call(functools.partial(expert_kernel, (tok_rows, width, experts...  123 us
    unnamed x5, local copies, waits for them, and re-layouts  4.25 us

profile of v7, /device:TPU:1, one launch (start us, length us, event | category | flops | bytes accessed | tf_op | source)
XLA Modules:
  0.0 128.2 jit_solution(14486515442829438529)
XLA Ops:
  0.6 123.4 %expert.1 = (bf16[448,128]{1,0:T(8,128)(2,1)S(1)}, f32[8,128]{1,0:T(8,128)S(1)}, bf16[160,3584]{1,0:T(8,128)(2,1)S(1)}, bf16[160,3584]{1,0:T(8,128)(2,1)S(1)}, bf16[160,3584]{1,0:T(8,128)(2,1)S(1)}) custom-call(bf16[128,3584]{1,0:T(8,128)(2,1)} %bitcast.28, bf16[128,3584]{1,0:T(8,128)(2,1)} %bitcast.29, s32[8,128]{1,0:T(8,128)} %bitcast.30, ...), custom_call_target="tpu_custom_call" | custom-call | tf_op jit(solution)/shard_map/expert/pallas_call | solution.py:586
  124.0 0.6 copy.17
  124.7 0.6 copy.18
  125.2 1.0 copy.19
  126.2 1.0 copy.20
  127.2 1.0 copy.21
